TPU v7x, 32 devices: a whole 2x2x4 slice. The times are simulated.
32 devices in a mesh: dp: 4 (over x, core), seq: 8 (over z, y).
Axes of the slice: x: 2, y: 2, z: 4, core: 2. Of those that a mesh axis runs over, the one named last changes fastest.
Arguments:
- inputs: bfloat16 [16, 1024, 768], P('dp', 'seq'), may hold values from -6 to 6
- memory: bfloat16 [16, 64, 768], P('dp', 'seq'), may hold values from -6 to 6
- patch_count: int32 [16], P('dp'), may hold values from 16 to 64, as said below
- cotangent: bfloat16 [16, 1024, 768], P('dp', 'seq'), may hold values from -6 to 6
- norm_self: float32 [768], replicated, may hold values from 0.5 to 1.5
- w_query: bfloat16 [768, 768], replicated, may hold values from -0.21875 to 0.21875
- w_key: bfloat16 [768, 768], replicated, may hold values from -0.21875 to 0.21875
- w_value: bfloat16 [768, 768], replicated, may hold values from -0.21875 to 0.21875
- w_out: bfloat16 [768, 768], replicated, may hold values from -3.0625 to 3.0625
- norm_cross: float32 [768], replicated, may hold values from 0.5 to 1.5
- c_query: bfloat16 [768, 768], replicated, may hold values from -0.21875 to 0.21875
- c_key: bfloat16 [768, 768], replicated, may hold values from -0.21875 to 0.21875
- c_value: bfloat16 [768, 768], replicated, may hold values from -0.21875 to 0.21875
- c_out: bfloat16 [768, 768], replicated, may hold values from -0.8125 to 0.8125
- norm_ffn: float32 [768], replicated, may hold values from 0.5 to 1.5
- w_gate: bfloat16 [768, 2048], replicated, may hold values from -0.21875 to 0.21875
- w_up: bfloat16 [768, 2048], replicated, may hold values from -0.21875 to 0.21875
- w_down: bfloat16 [2048, 768], replicated, may hold values from -0.125 to 0.125
Outputs:
- block_output: float32 [16, 1024, 768], P('dp', 'seq')
- input_grad: float32 [16, 1024, 768], P('dp', 'seq')
- memory_grad: float32 [16, 64, 768], P('dp', 'seq')
- grad_norm_self: float32 [768], P('seq')
- grad_w_query: float32 [768, 768], P('seq', 'dp')
- grad_w_key: float32 [768, 768], P('seq', 'dp')
- grad_w_value: float32 [768, 768], P('seq', 'dp')
- grad_w_out: float32 [768, 768], P('seq', 'dp')
- grad_norm_cross: float32 [768], P('seq')
- grad_c_query: float32 [768, 768], P('seq', 'dp')
- grad_c_key: float32 [768, 768], P('seq', 'dp')
- grad_c_value: float32 [768, 768], P('seq', 'dp')
- grad_c_out: float32 [768, 768], P('seq', 'dp')
- grad_norm_ffn: float32 [768], P('seq')
- grad_w_gate: float32 [768, 2048], P('seq', 'dp')
- grad_w_up: float32 [768, 2048], P('seq', 'dp')
- grad_w_down: float32 [2048, 768], P('seq', 'dp')
Inputs may be any that keep to these rules, and one draw needn't show every extreme that they name: Patches 0 to patch_count - 1 of a chart are valid, the others masked; some chart has all 64 valid and some has 16.
All inputs are finite; a program needn't handle non-finite values.
Results may differ from a plain program's by a relative error of at most 0.02.
Values may be sent and summed in bfloat16 or wider, within the bound.
No kernel may reach another device: no remote copies, remote signals or barrier semaphores. Data moves between devices by JAX's collectives and lax.ppermute only.
A program may use at most 896 MiB of HBM per device.

v0:
```python
import jax
import jax.numpy as jnp
from jax import lax
from jax.sharding import PartitionSpec as P

H = 12


EPSILON = 1e-06
NEGATIVE = -1e30


def norm_scale(values, gain):
    return values * lax.rsqrt(jnp.mean(values * values, axis=-1, keepdims=True) + EPSILON) * gain


def gelu_tanh(values):
    return (
        0.5
        * values
        * (1.0 + jnp.tanh(0.7978845608028654 * (values + 0.044715 * values * values * values)))
    )


def gated(gate, upward):
    return gelu_tanh(gate) * upward


def matmul(left, right):
    return jnp.dot(left, right, preferred_element_type=jnp.float32)


def left_product(left, right):
    return lax.dot_general(
        left, right, (((0,), (0,)), ((), ())), preferred_element_type=jnp.float32
    )


def right_product(left, right):
    return lax.dot_general(
        left, right, (((1,), (1,)), ((), ())), preferred_element_type=jnp.float32
    )


def project(rows_in, weight, charts):
    return matmul(rows_in, weight).astype(jnp.bfloat16).reshape(charts, -1, weight.shape[1])


def to_items(array, heads):
    charts, count, width = array.shape
    head = width // heads
    return (
        array.reshape(charts, count, heads, head)
        .transpose(0, 2, 1, 3)
        .reshape(charts * heads, count * head)
    )


def from_items(array, heads, head):
    total, flat = array.shape
    count = flat // head
    return (
        array.reshape(total // heads, heads, count, head)
        .transpose(0, 2, 1, 3)
        .reshape(total // heads, count, heads * head)
    )


def causal_mask(start, block, limit):
    places = start + jnp.arange(block, dtype=jnp.int32)
    return (places[:, None] >= jnp.arange(limit, dtype=jnp.int32)[None, :])[None]


def block_scores(part, keys, scale, allow, start, block, limit):
    raw = jnp.einsum("iqd,ikd->iqk", part, keys, preferred_element_type=jnp.float32)
    return jnp.where(allow(start, block, limit), raw * scale, NEGATIVE)


def attend_forward(queries, keys, values, allow, causal):
    total, length, head = queries.shape
    block = min(512, length)
    scale = head ** (-0.5)
    results = []
    sums = []
    for start in range(0, length, block):
        limit = start + block if causal else keys.shape[1]
        scores = block_scores(
            queries[:, start : start + block], keys[:, :limit], scale, allow, start, block, limit
        )
        highest = jnp.max(scores, axis=2, keepdims=True)
        shifted = jnp.exp(scores - highest)
        whole = jnp.sum(shifted, axis=2, keepdims=True)
        weights = (shifted / whole).astype(jnp.bfloat16)
        attended = jnp.einsum(
            "iqk,ikd->iqd", weights, values[:, :limit], preferred_element_type=jnp.float32
        )
        results.append(attended.astype(jnp.bfloat16))
        sums.append(highest + jnp.log(whole))
    return (jnp.concatenate(results, 1), jnp.concatenate(sums, 1))


def attend_backward(queries, keys, values, sums, grad_out, allow, causal):
    total, length, head = queries.shape
    key_total = keys.shape[1]
    block = min(512, length)
    scale = head ** (-0.5)
    query_parts = []
    key_terms = []
    value_terms = []
    for start in range(0, length, block):
        limit = start + block if causal else key_total
        part = queries[:, start : start + block]
        grad_part = grad_out[:, start : start + block]
        near_keys = keys[:, :limit]
        near_values = values[:, :limit]
        scores = block_scores(part, near_keys, scale, allow, start, block, limit)
        weights = jnp.exp(scores - sums[:, start : start + block])
        value_terms.append(
            jnp.einsum(
                "iqk,iqd->ikd",
                weights.astype(jnp.bfloat16),
                grad_part,
                preferred_element_type=jnp.float32,
            )
        )
        weight_grad = jnp.einsum(
            "iqd,ikd->iqk", grad_part, near_values, preferred_element_type=jnp.float32
        )
        row_dot = jnp.sum(weights * weight_grad, axis=2, keepdims=True)
        score_grad = (weights * (weight_grad - row_dot)).astype(jnp.bfloat16)
        query_parts.append(
            jnp.einsum("iqk,ikd->iqd", score_grad, near_keys, preferred_element_type=jnp.float32)
            * scale
        )
        key_terms.append(
            jnp.einsum("iqk,iqd->ikd", score_grad, part, preferred_element_type=jnp.float32) * scale
        )
    if causal:
        key_pieces = []
        value_pieces = []
        count = len(key_terms)
        for index in range(count):
            low_edge = index * block
            key_piece = key_terms[index][:, low_edge : low_edge + block]
            value_piece = value_terms[index][:, low_edge : low_edge + block]
            for later in range(index + 1, count):
                key_piece = key_piece + key_terms[later][:, low_edge : low_edge + block]
                value_piece = value_piece + value_terms[later][:, low_edge : low_edge + block]
            key_pieces.append(key_piece)
            value_pieces.append(value_piece)
        key_grad = jnp.concatenate(key_pieces, 1)
        value_grad = jnp.concatenate(value_pieces, 1)
    else:
        key_grad = key_terms[0]
        value_grad = value_terms[0]
        for index in range(1, len(key_terms)):
            key_grad = key_grad + key_terms[index]
            value_grad = value_grad + value_terms[index]
    return (jnp.concatenate(query_parts, 1), key_grad, value_grad)


def local(
    inputs,
    memory,
    patch_count,
    cotangent,
    norm_self,
    w_query,
    w_key,
    w_value,
    w_out,
    norm_cross,
    c_query,
    c_key,
    c_value,
    c_out,
    norm_ffn,
    w_gate,
    w_up,
    w_down,
):
    local_charts, tokens, width = inputs.shape
    local_patches = memory.shape[1]
    heads = H
    head = width // heads
    seq_devices = lax.axis_size("seq")
    dp_devices = lax.axis_size("dp")
    per_batch = seq_devices // 4
    items = per_batch * heads // seq_devices
    length = tokens * seq_devices
    patches = local_patches * seq_devices
    rows = per_batch * tokens
    memory_rows = per_batch * local_patches
    first_item = lax.axis_index("seq") * items
    owners = (first_item + jnp.arange(items, dtype=jnp.int32)) // heads
    owner_table = owners[:, None] == jnp.arange(per_batch, dtype=jnp.int32)[None, :]
    params = (
        norm_self,
        w_query,
        w_key,
        w_value,
        w_out,
        norm_cross,
        c_query,
        c_key,
        c_value,
        c_out,
        norm_ffn,
        w_gate,
        w_up,
        w_down,
    )
    grads = [jnp.zeros(p.shape, jnp.float32) for p in params]
    outputs = []
    input_grads = []
    memory_grads = []
    for lower in range(0, local_charts, per_batch):
        current = inputs[lower : lower + per_batch].astype(jnp.float32)
        memory_flat = memory[lower : lower + per_batch].reshape(memory_rows, width)
        counts_now = patch_count[lower : lower + per_batch]
        item_counts = jnp.sum(jnp.where(owner_table, counts_now[None, :], 0), axis=1)

        def masked(start, block, limit):
            return jnp.arange(limit, dtype=jnp.int32)[None, None, :] < item_counts[:, None, None]

        normed_one, pull_one = jax.vjp(norm_scale, current, norm_self)
        rounded_one = normed_one.astype(jnp.bfloat16).reshape(rows, width)
        query_self = to_items(project(rounded_one, w_query, per_batch), heads)
        key_self = to_items(project(rounded_one, w_key, per_batch), heads)
        value_self = to_items(project(rounded_one, w_value, per_batch), heads)
        memory_keys = to_items(project(memory_flat, c_key, per_batch), heads)
        memory_values = to_items(project(memory_flat, c_value, per_batch), heads)
        query_self, key_self, value_self = (
            lax.all_to_all(query_self, "seq", split_axis=0, concat_axis=1, tiled=True),
            lax.all_to_all(key_self, "seq", split_axis=0, concat_axis=1, tiled=True),
            lax.all_to_all(value_self, "seq", split_axis=0, concat_axis=1, tiled=True),
        )
        self_queries = query_self.reshape(items, length, head)
        self_keys = key_self.reshape(items, length, head)
        self_values = value_self.reshape(items, length, head)
        mixed_heads, sums_self = attend_forward(
            self_queries, self_keys, self_values, causal_mask, True
        )
        mixed = lax.all_to_all(
            mixed_heads.reshape(items, length * head),
            "seq",
            split_axis=1,
            concat_axis=0,
            tiled=True,
        )
        mixed = from_items(mixed, heads, head).reshape(rows, width)
        after_self = current + matmul(mixed, w_out).reshape(per_batch, tokens, width)
        normed_two, pull_two = jax.vjp(norm_scale, after_self, norm_cross)
        rounded_two = normed_two.astype(jnp.bfloat16).reshape(rows, width)
        query_cross = to_items(project(rounded_two, c_query, per_batch), heads)
        query_cross, memory_keys, memory_values = (
            lax.all_to_all(query_cross, "seq", split_axis=0, concat_axis=1, tiled=True),
            lax.all_to_all(memory_keys, "seq", split_axis=0, concat_axis=1, tiled=True),
            lax.all_to_all(memory_values, "seq", split_axis=0, concat_axis=1, tiled=True),
        )
        cross_queries = query_cross.reshape(items, length, head)
        cross_keys = memory_keys.reshape(items, patches, head)
        cross_values = memory_values.reshape(items, patches, head)
        fetched_heads, sums_cross = attend_forward(
            cross_queries, cross_keys, cross_values, masked, False
        )
        fetched = lax.all_to_all(
            fetched_heads.reshape(items, length * head),
            "seq",
            split_axis=1,
            concat_axis=0,
            tiled=True,
        )
        fetched = from_items(fetched, heads, head).reshape(rows, width)
        after_cross = after_self + matmul(fetched, c_out).reshape(per_batch, tokens, width)
        normed_three, pull_three = jax.vjp(norm_scale, after_cross, norm_ffn)
        rounded_three = normed_three.astype(jnp.bfloat16).reshape(rows, width)
        gate = matmul(rounded_three, w_gate)
        upward = matmul(rounded_three, w_up)
        hidden_full, pull_gate = jax.vjp(gated, gate, upward)
        hidden = hidden_full.astype(jnp.bfloat16)
        outputs.append(after_cross + matmul(hidden, w_down).reshape(per_batch, tokens, width))
        upstream = cotangent[lower : lower + per_batch]
        flowing = upstream.reshape(rows, width)
        grads[13] = grads[13] + left_product(hidden, flowing)
        gate_grad, up_grad = pull_gate(right_product(flowing, w_down))
        gate_grad = gate_grad.astype(jnp.bfloat16)
        up_grad = up_grad.astype(jnp.bfloat16)
        grads[11] = grads[11] + left_product(rounded_three, gate_grad)
        grads[12] = grads[12] + left_product(rounded_three, up_grad)
        back_three = right_product(gate_grad, w_gate) + right_product(up_grad, w_up)
        into_cross, gain_three = pull_three(back_three.reshape(per_batch, tokens, width))
        grads[10] = grads[10] + gain_three
        cross_grad = upstream.astype(jnp.float32) + into_cross
        flowing = cross_grad.reshape(rows, width).astype(jnp.bfloat16)
        grads[9] = grads[9] + left_product(fetched, flowing)
        fetched_grad = to_items(
            right_product(flowing, c_out).astype(jnp.bfloat16).reshape(per_batch, tokens, width),
            heads,
        )
        fetched_grad = lax.all_to_all(
            fetched_grad, "seq", split_axis=0, concat_axis=1, tiled=True
        ).reshape(items, length, head)
        cross_dq, cross_dk, cross_dv = attend_backward(
            cross_queries, cross_keys, cross_values, sums_cross, fetched_grad, masked, False
        )
        back_query, back_keys, back_values = (
            lax.all_to_all(
                cross_dq.astype(jnp.bfloat16).reshape(items, length * head),
                "seq",
                split_axis=1,
                concat_axis=0,
                tiled=True,
            ),
            lax.all_to_all(
                cross_dk.astype(jnp.bfloat16).reshape(items, patches * head),
                "seq",
                split_axis=1,
                concat_axis=0,
                tiled=True,
            ),
            lax.all_to_all(
                cross_dv.astype(jnp.bfloat16).reshape(items, patches * head),
                "seq",
                split_axis=1,
                concat_axis=0,
                tiled=True,
            ),
        )
        back_query = from_items(back_query, heads, head).reshape(rows, width)
        back_keys = from_items(back_keys, heads, head).reshape(memory_rows, width)
        back_values = from_items(back_values, heads, head).reshape(memory_rows, width)
        grads[6] = grads[6] + left_product(rounded_two, back_query)
        grads[7] = grads[7] + left_product(memory_flat, back_keys)
        grads[8] = grads[8] + left_product(memory_flat, back_values)
        memory_term = right_product(back_keys, c_key) + right_product(back_values, c_value)
        memory_grads.append(memory_term.reshape(per_batch, local_patches, width))
        into_self, gain_two = pull_two(
            right_product(back_query, c_query).reshape(per_batch, tokens, width)
        )
        grads[5] = grads[5] + gain_two
        self_grad = cross_grad + into_self
        flowing = self_grad.reshape(rows, width).astype(jnp.bfloat16)
        grads[4] = grads[4] + left_product(mixed, flowing)
        mixed_grad = to_items(
            right_product(flowing, w_out).astype(jnp.bfloat16).reshape(per_batch, tokens, width),
            heads,
        )
        mixed_grad = lax.all_to_all(
            mixed_grad, "seq", split_axis=0, concat_axis=1, tiled=True
        ).reshape(items, length, head)
        self_dq, self_dk, self_dv = attend_backward(
            self_queries, self_keys, self_values, sums_self, mixed_grad, causal_mask, True
        )
        back_query, back_keys, back_values = (
            lax.all_to_all(
                self_dq.astype(jnp.bfloat16).reshape(items, length * head),
                "seq",
                split_axis=1,
                concat_axis=0,
                tiled=True,
            ),
            lax.all_to_all(
                self_dk.astype(jnp.bfloat16).reshape(items, length * head),
                "seq",
                split_axis=1,
                concat_axis=0,
                tiled=True,
            ),
            lax.all_to_all(
                self_dv.astype(jnp.bfloat16).reshape(items, length * head),
                "seq",
                split_axis=1,
                concat_axis=0,
                tiled=True,
            ),
        )
        back_query = from_items(back_query, heads, head).reshape(rows, width)
        back_keys = from_items(back_keys, heads, head).reshape(rows, width)
        back_values = from_items(back_values, heads, head).reshape(rows, width)
        grads[1] = grads[1] + left_product(rounded_one, back_query)
        grads[2] = grads[2] + left_product(rounded_one, back_keys)
        grads[3] = grads[3] + left_product(rounded_one, back_values)
        back_one = (
            right_product(back_query, w_query)
            + right_product(back_keys, w_key)
            + right_product(back_values, w_value)
        )
        into_input, gain_one = pull_one(back_one.reshape(per_batch, tokens, width))
        grads[0] = grads[0] + gain_one
        input_grads.append(self_grad + into_input)
    shares = (
        lax.psum_scatter(grads[0], "seq", scatter_dimension=0, tiled=True),
        lax.psum_scatter(grads[1], "seq", scatter_dimension=0, tiled=True),
        lax.psum_scatter(grads[2], "seq", scatter_dimension=0, tiled=True),
        lax.psum_scatter(grads[3], "seq", scatter_dimension=0, tiled=True),
        lax.psum_scatter(grads[4], "seq", scatter_dimension=0, tiled=True),
        lax.psum_scatter(grads[5], "seq", scatter_dimension=0, tiled=True),
        lax.psum_scatter(grads[6], "seq", scatter_dimension=0, tiled=True),
        lax.psum_scatter(grads[7], "seq", scatter_dimension=0, tiled=True),
        lax.psum_scatter(grads[8], "seq", scatter_dimension=0, tiled=True),
        lax.psum_scatter(grads[9], "seq", scatter_dimension=0, tiled=True),
        lax.psum_scatter(grads[10], "seq", scatter_dimension=0, tiled=True),
        lax.psum_scatter(grads[11], "seq", scatter_dimension=0, tiled=True),
        lax.psum_scatter(grads[12], "seq", scatter_dimension=0, tiled=True),
        lax.psum_scatter(grads[13], "seq", scatter_dimension=0, tiled=True),
    )
    gain_rows = shares[0].shape[0]
    spread_self = jnp.broadcast_to(shares[0][:, None], (gain_rows, dp_devices))
    spread_cross = jnp.broadcast_to(shares[5][:, None], (gain_rows, dp_devices))
    spread_ffn = jnp.broadcast_to(shares[10][:, None], (gain_rows, dp_devices))
    totals = (
        lax.psum_scatter(
            spread_self.astype(jnp.bfloat16), "dp", scatter_dimension=1, tiled=True
        ).astype(jnp.float32),
        lax.psum_scatter(
            shares[1].astype(jnp.bfloat16), "dp", scatter_dimension=1, tiled=True
        ).astype(jnp.float32),
        lax.psum_scatter(
            shares[2].astype(jnp.bfloat16), "dp", scatter_dimension=1, tiled=True
        ).astype(jnp.float32),
        lax.psum_scatter(
            shares[3].astype(jnp.bfloat16), "dp", scatter_dimension=1, tiled=True
        ).astype(jnp.float32),
        lax.psum_scatter(
            shares[4].astype(jnp.bfloat16), "dp", scatter_dimension=1, tiled=True
        ).astype(jnp.float32),
        lax.psum_scatter(
            spread_cross.astype(jnp.bfloat16), "dp", scatter_dimension=1, tiled=True
        ).astype(jnp.float32),
        lax.psum_scatter(
            shares[6].astype(jnp.bfloat16), "dp", scatter_dimension=1, tiled=True
        ).astype(jnp.float32),
        lax.psum_scatter(
            shares[7].astype(jnp.bfloat16), "dp", scatter_dimension=1, tiled=True
        ).astype(jnp.float32),
        lax.psum_scatter(
            shares[8].astype(jnp.bfloat16), "dp", scatter_dimension=1, tiled=True
        ).astype(jnp.float32),
        lax.psum_scatter(
            shares[9].astype(jnp.bfloat16), "dp", scatter_dimension=1, tiled=True
        ).astype(jnp.float32),
        lax.psum_scatter(
            spread_ffn.astype(jnp.bfloat16), "dp", scatter_dimension=1, tiled=True
        ).astype(jnp.float32),
        lax.psum_scatter(
            shares[11].astype(jnp.bfloat16), "dp", scatter_dimension=1, tiled=True
        ).astype(jnp.float32),
        lax.psum_scatter(
            shares[12].astype(jnp.bfloat16), "dp", scatter_dimension=1, tiled=True
        ).astype(jnp.float32),
        lax.psum_scatter(
            shares[13].astype(jnp.bfloat16), "dp", scatter_dimension=1, tiled=True
        ).astype(jnp.float32),
    )
    return (
        jnp.concatenate(outputs, 0),
        jnp.concatenate(input_grads, 0),
        jnp.concatenate(memory_grads, 0),
        totals[0].reshape(gain_rows),
        totals[1],
        totals[2],
        totals[3],
        totals[4],
        totals[5].reshape(gain_rows),
        totals[6],
        totals[7],
        totals[8],
        totals[9],
        totals[10].reshape(gain_rows),
        totals[11],
        totals[12],
        totals[13],
    )


def solution(mesh):
    in_specs = (
        P("dp", "seq", None),
        P("dp", "seq", None),
        P("dp"),
        P("dp", "seq", None),
        P(),
        P(),
        P(),
        P(),
        P(),
        P(),
        P(),
        P(),
        P(),
        P(),
        P(),
        P(),
        P(),
        P(),
    )
    out_specs = (
        P("dp", "seq", None),
        P("dp", "seq", None),
        P("dp", "seq", None),
        P("seq"),
        P("seq", "dp"),
        P("seq", "dp"),
        P("seq", "dp"),
        P("seq", "dp"),
        P("seq"),
        P("seq", "dp"),
        P("seq", "dp"),
        P("seq", "dp"),
        P("seq", "dp"),
        P("seq"),
        P("seq", "dp"),
        P("seq", "dp"),
        P("seq", "dp"),
    )
    return jax.shard_map(local, mesh=mesh, in_specs=in_specs, out_specs=out_specs, check_vma=False)
```

profile of v0, /device:TPU:0, one launch (start us, length us, event | category | flops | bytes accessed | tf_op | source)
XLA Modules:
  0.0 1713.5 jit_solution(6952419895373253938)
XLA Ops:
  492.4 22.6 %all-to-all-done.22 = bf16[8,3,8192]{2,1,0:T(4,128)(2,1)S(1)} async-done(((bf16[8,3,8192]{2,1,0:T(4,128)(2,1)}), bf16[8,3,8192]{2,1,0:T(4,128)(2,1)S(1)}, u32[]{:S(2)}, u32[]{:S(2)}) %all-to-all-start.22) | async-done | bytes 393248 | tf_op jit(solution)/shard_map/all_to_all | solution.py:301
  574.1 20.4 %all-to-all-done.23 = bf16[3,8,8192]{2,0,1:T(4,128)(2,1)} async-done(((bf16[3,8,8192]{2,0,1:T(4,128)(2,1)}), bf16[3,8,8192]{2,0,1:T(4,128)(2,1)}, u32[]{:S(2)}, u32[]{:S(2)}) %all-to-all-start.23) | async-done | bytes 393248 | tf_op jit(solution)/shard_map/all_to_all | solution.py:308
  663.7 11.2 all-to-all-done.24
  802.1 9.5 all-to-all-done.19
  819.6 17.2 %all-to-all-done.25 = bf16[3,8,8192]{2,0,1:T(4,128)(2,1)} async-done(((bf16[3,8,8192]{2,0,1:T(4,128)(2,1)}), bf16[3,8,8192]{2,0,1:T(4,128)(2,1)}, u32[]{:S(2)}, u32[]{:S(2)}) %all-to-all-start.25) | async-done | bytes 393248 | tf_op jit(solution)/shard_map/all_to_all | solution.py:356
  869.4 10.4 reduce-scatter.47.cloned.1.call-done
  884.0 67.4 %reduce-scatter.45.cloned.1.call-done = f32[96,768]{1,0:T(8,128)} async-done(((f32[768,768]{1,0:T(8,128)}), f32[96,768]{1,0:T(8,128)}) %reduce-scatter.45.cloned.1.call-update) | async-done | bytes 294928 | tf_op jit(solution)/shard_map/reduce_scatter | solution.py:396
  956.4 66.6 %reduce-scatter.43.cloned.1.call-done = f32[96,768]{1,0:T(8,128)} async-done(((f32[768,768]{1,0:T(8,128)}), f32[96,768]{1,0:T(8,128)}) %reduce-scatter.43.cloned.1.call-update) | async-done | bytes 294928 | tf_op jit(solution)/shard_map/reduce_scatter | solution.py:395
  1025.8 69.0 %reduce-scatter.41.cloned.1.call-done = f32[96,768]{1,0:T(8,128)} async-done(((f32[768,768]{1,0:T(8,128)}), f32[96,768]{1,0:T(8,128)}) %reduce-scatter.41.cloned.1.call-update) | async-done | bytes 294928 | tf_op jit(solution)/shard_map/reduce_scatter | solution.py:394
  1100.1 115.3 %reduce-scatter.65.cloned.1.call-done = f32[256,768]{1,0:T(8,128)} async-done(((f32[2048,768]{1,0:T(8,128)}), f32[256,768]{1,0:T(8,128)}) %reduce-scatter.65.cloned.1.call-update) | async-done | bytes 786448 | tf_op jit(solution)/shard_map/reduce_scatter | solution.py:406
  1222.1 114.0 %reduce-scatter.61.cloned.1.call-done = f32[96,2048]{1,0:T(8,128)} async-done(((f32[768,2048]{1,0:T(8,128)}), f32[96,2048]{1,0:T(8,128)}) %reduce-scatter.61.cloned.1.call-update) | async-done | bytes 786448 | tf_op jit(solution)/shard_map/reduce_scatter | solution.py:405
  1342.2 37.2 %all-reduce.6 = (bf16[768]{0:T(1024)(128)(2,1)S(1)}, bf16[768]{0:T(1024)(128)(2,1)S(1)}, bf16[768]{0:T(1024)(128)(2,1)S(1)}) all-reduce(f32[768]{0:T(1024)S(1)} %add.404, f32[768]{0:T(1024)S(1)} %add.409, f32[768]{0:T(1024)S(1)} %add.416), channel_id=2, replica_groups=mesh['dp'=4,'seq'=8] {'seq'}, use_global_device_ids=true, to_apply=%region_40.41.clone | all-reduce | flops 2304 | bytes 13824
  1386.9 70.5 %reduce-scatter.57.cloned.1.call-done = f32[96,2048]{1,0:T(8,128)} async-done(((f32[768,2048]{1,0:T(8,128)}), f32[96,2048]{1,0:T(8,128)}) %reduce-scatter.57.cloned.1.call-update) | async-done | bytes 786448 | tf_op jit(solution)/shard_map/reduce_scatter | solution.py:404
  1463.4 15.2 reduce-scatter.81.cloned.1.call-done
  1480.1 20.7 %reduce-scatter.53.cloned.1.call-done = bf16[96,192]{0,1:T(8,128)(2,1)} async-done(((bf16[96,768]{0,1:T(8,128)(2,1)}), bf16[96,192]{0,1:T(8,128)(2,1)}) %reduce-scatter.53.cloned.1.call-update) | async-done | bytes 36880 | tf_op jit(solution)/shard_map/reduce_scatter | solution.py:437
  1502.3 20.5 %reduce-scatter.51.cloned.1.call-done = bf16[96,192]{0,1:T(8,128)(2,1)} async-done(((bf16[96,768]{0,1:T(8,128)(2,1)}), bf16[96,192]{0,1:T(8,128)(2,1)}) %reduce-scatter.51.cloned.1.call-update) | async-done | bytes 36880 | tf_op jit(solution)/shard_map/reduce_scatter | solution.py:434
  1524.4 20.5 %reduce-scatter.75.cloned.1.call-done = bf16[192,96]{1,0:T(8,128)(2,1)} async-done(((bf16[768,96]{1,0:T(8,128)(2,1)}), bf16[192,96]{1,0:T(8,128)(2,1)}) %reduce-scatter.75.cloned.1.call-update) | async-done | bytes 36880
  1546.5 20.5 %reduce-scatter.73.cloned.1.call-done = bf16[192,96]{1,0:T(8,128)(2,1)} async-done(((bf16[768,96]{1,0:T(8,128)(2,1)}), bf16[192,96]{1,0:T(8,128)(2,1)}) %reduce-scatter.73.cloned.1.call-update) | async-done | bytes 36880
  1568.5 21.1 %reduce-scatter.71.cloned.1.call-done = bf16[192,96]{1,0:T(8,128)(2,1)} async-done(((bf16[768,96]{1,0:T(8,128)(2,1)}), bf16[192,96]{1,0:T(8,128)(2,1)}) %reduce-scatter.71.cloned.1.call-update) | async-done | bytes 36880
  1591.1 21.1 %reduce-scatter.69.cloned.1.call-done = bf16[192,96]{1,0:T(8,128)(2,1)} async-done(((bf16[768,96]{1,0:T(8,128)(2,1)}), bf16[192,96]{1,0:T(8,128)(2,1)}) %reduce-scatter.69.cloned.1.call-update) | async-done | bytes 36880
  1613.7 21.2 %reduce-scatter.67.cloned.1.call-done = bf16[192,96]{1,0:T(8,128)(2,1)} async-done(((bf16[768,96]{1,0:T(8,128)(2,1)}), bf16[192,96]{1,0:T(8,128)(2,1)}) %reduce-scatter.67.cloned.1.call-update) | async-done | bytes 36880
  1636.5 21.6 %reduce-scatter.83.cloned.1.call-done = bf16[192,256]{1,0:T(8,128)(2,1)} async-done(((bf16[768,256]{1,0:T(8,128)(2,1)}), bf16[192,256]{1,0:T(8,128)(2,1)}) %reduce-scatter.83.cloned.1.call-update) | async-done | bytes 98320
  1659.9 21.6 %reduce-scatter.63.cloned.1.call-done = bf16[96,512]{1,0:T(8,128)(2,1)} async-done(((bf16[96,2048]{1,0:T(8,128)(2,1)}), bf16[96,512]{1,0:T(8,128)(2,1)}) %reduce-scatter.63.cloned.1.call-update) | async-done | bytes 98320 | tf_op jit(solution)/shard_map/reduce_scatter | solution.py:449
  1683.1 21.7 %reduce-scatter.59.cloned.1.call-done = bf16[96,512]{1,0:T(8,128)(2,1)} async-done(((bf16[96,2048]{1,0:T(8,128)(2,1)}), bf16[96,512]{1,0:T(8,128)(2,1)}) %reduce-scatter.59.cloned.1.call-update) | async-done | bytes 98320 | tf_op jit(solution)/shard_map/reduce_scatter | solution.py:446
  (955 shorter events, 838.0 us)
Async XLA Ops:
  21.1 30.1 %all-to-all-start = ((bf16[8,3,8192]{2,1,0:T(4,128)(2,1)}), bf16[8,3,8192]{2,1,0:T(4,128)(2,1)}, u32[]{:S(2)}, u32[]{:S(2)}) async-start(bf16[8,3,8192]{2,1,0:T(4,128)(2,1)} %all_to_all.368), calls=%async_computation | async-start | bytes 1048576 | tf_op jit(solution)/shard_map/all_to_all | solution.py:234
  71.2 31.7 %all-to-all-start.5 = ((bf16[8,3,512]{2,1,0:T(4,128)(2,1)}), bf16[8,3,512]{2,1,0:T(4,128)(2,1)}, u32[]{:S(2)}, u32[]{:S(2)}) async-start(bf16[8,3,512]{2,1,0:T(4,128)(2,1)} %all_to_all.383), calls=%async_computation.5 | async-start | bytes 65536 | tf_op jit(solution)/shard_map/all_to_all | solution.py:258
  433.9 427.8 %reduce-scatter.55.cloned.1.call-start = ((), (), s32[]{:S(2)}) async-start(), calls=%async_computation.61 | async-start | bytes 2654208 | tf_op jit(solution)/shard_map/reduce_scatter | solution.py:402
  520.9 342.8 %reduce-scatter.79.cloned.1.call-start = ((), (), s32[]{:S(2)}) async-start(), calls=%async_computation.73 | async-start | bytes 2654208
  552.4 313.2 %reduce-scatter.77.cloned.1.call-start = ((), (), s32[]{:S(2)}) async-start(), calls=%async_computation.72 | async-start | bytes 2654208
  572.6 294.9 %reduce-scatter.49.cloned.1.call-start = ((), (), s32[]{:S(2)}) async-start(), calls=%async_computation.58 | async-start | bytes 2654208 | tf_op jit(solution)/shard_map/reduce_scatter | solution.py:399
  610.2 269.6 %reduce-scatter.47.cloned.1.call-start = ((), (), s32[]{:S(2)}) async-start(), calls=%async_computation.57 | async-start | bytes 2654208 | tf_op jit(solution)/shard_map/reduce_scatter | solution.py:397
  697.0 254.3 %reduce-scatter.45.cloned.1.call-start = ((), (), s32[]{:S(2)}) async-start(), calls=%async_computation.56 | async-start | bytes 2654208 | tf_op jit(solution)/shard_map/reduce_scatter | solution.py:396
  766.7 256.3 %reduce-scatter.43.cloned.1.call-start = ((), (), s32[]{:S(2)}) async-start(), calls=%async_computation.55 | async-start | bytes 2654208 | tf_op jit(solution)/shard_map/reduce_scatter | solution.py:395
  816.8 278.0 %reduce-scatter.41.cloned.1.call-start = ((), (), s32[]{:S(2)}) async-start(), calls=%async_computation.54 | async-start | bytes 2654208 | tf_op jit(solution)/shard_map/reduce_scatter | solution.py:394
  842.8 372.7 %reduce-scatter.65.cloned.1.call-start = ((), (), s32[]{:S(2)}) async-start(), calls=%async_computation.66 | async-start | bytes 7077888 | tf_op jit(solution)/shard_map/reduce_scatter | solution.py:406
  849.1 486.9 %reduce-scatter.61.cloned.1.call-start = ((), (), s32[]{:S(2)}) async-start(), calls=%async_computation.64 | async-start | bytes 7077888 | tf_op jit(solution)/shard_map/reduce_scatter | solution.py:405
  855.4 601.9 %reduce-scatter.57.cloned.1.call-start = ((), (), s32[]{:S(2)}) async-start(), calls=%async_computation.62 | async-start | bytes 7077888 | tf_op jit(solution)/shard_map/reduce_scatter | solution.py:404
  861.7 616.9 %reduce-scatter.81.cloned.1.call-start = ((), (), s32[]{:S(2)}) async-start(), calls=%async_computation.74 | async-start | bytes 245760
  863.6 637.1 %reduce-scatter.53.cloned.1.call-start = ((), (), s32[]{:S(2)}) async-start(), calls=%async_computation.60 | async-start | bytes 245760 | tf_op jit(solution)/shard_map/reduce_scatter | solution.py:437
  865.5 657.3 %reduce-scatter.51.cloned.1.call-start = ((), (), s32[]{:S(2)}) async-start(), calls=%async_computation.59 | async-start | bytes 245760 | tf_op jit(solution)/shard_map/reduce_scatter | solution.py:434
  867.5 677.4 %reduce-scatter.75.cloned.1.call-start = ((), (), s32[]{:S(2)}) async-start(), calls=%async_computation.71 | async-start | bytes 245760
  869.4 697.6 %reduce-scatter.73.cloned.1.call-start = ((), (), s32[]{:S(2)}) async-start(), calls=%async_computation.70 | async-start | bytes 245760
  881.6 707.9 %reduce-scatter.71.cloned.1.call-start = ((), (), s32[]{:S(2)}) async-start(), calls=%async_computation.69 | async-start | bytes 245760
  953.2 659.0 %reduce-scatter.69.cloned.1.call-start = ((), (), s32[]{:S(2)}) async-start(), calls=%async_computation.68 | async-start | bytes 245760
  1024.9 610.1 %reduce-scatter.67.cloned.1.call-start = ((), (), s32[]{:S(2)}) async-start(), calls=%async_computation.67 | async-start | bytes 245760
  1096.6 561.6 %reduce-scatter.83.cloned.1.call-start = ((), (), s32[]{:S(2)}) async-start(), calls=%async_computation.75 | async-start | bytes 491520
  1217.6 463.9 %reduce-scatter.63.cloned.1.call-start = ((), (), s32[]{:S(2)}) async-start(), calls=%async_computation.65 | async-start | bytes 491520 | tf_op jit(solution)/shard_map/reduce_scatter | solution.py:449
  1338.0 366.9 %reduce-scatter.59.cloned.1.call-start = ((), (), s32[]{:S(2)}) async-start(), calls=%async_computation.63 | async-start | bytes 491520 | tf_op jit(solution)/shard_map/reduce_scatter | solution.py:446
  (244 other events, 3830.1 us)
Sparse Core Ops, SparseCore 0:
  475.6 75.8 reduce-scatter.54
  555.0 77.2 reduce-scatter.78
  635.8 82.2 reduce-scatter.76
  721.4 83.2 reduce-scatter.48
  808.1 71.6 reduce-scatter.46
  883.2 68.1 reduce-scatter.44
  954.9 68.1 reduce-scatter.42
  1026.5 68.1 reduce-scatter.40
  1098.4 117.0 reduce-scatter.64
  1218.9 117.1 reduce-scatter.60
  1339.6 117.6 reduce-scatter.56
  1459.6 18.8 reduce-scatter.80
  1481.0 19.7 reduce-scatter.52
  1503.1 19.7 reduce-scatter.50
  1525.1 19.7 reduce-scatter.74
  1547.2 19.7 reduce-scatter.72
  1569.8 19.7 reduce-scatter.70
  1592.4 19.7 reduce-scatter.68
  1615.2 19.7 reduce-scatter.66
  1637.3 20.7 reduce-scatter.82
  1660.7 20.7 reduce-scatter.62
  1684.0 20.7 reduce-scatter.58
where the time goes:
time: 1730 us; the launch traced here: 1710 us
  waiting for transfers between devices  896 us (52%)
  local copies, waits for them, and re-layouts  308 us (18%)
  matrix products  205 us (12%)
  starting transfers between devices  157 us (9%)
  other arithmetic  76.1 us (4%)
  blocking collectives  52.8 us (3%)
  between operations  18.5 us (1%)
    unnamed x31, waiting for transfers between devices  142 us
    reduce_scatter x1, waiting for transfers between devices, local(): lax.psum_scatter(grads[13], 'seq', scatter_dimension=0, tiled=True)  115 us
    reduce_scatter x1, waiting for transfers between devices, local(): lax.psum_scatter(grads[12], 'seq', scatter_dimension=0, tiled=True)  114 us
    reduce_scatter x1, waiting for transfers between devices, local(): lax.psum_scatter(grads[11], 'seq', scatter_dimension=0, tiled=True)  70.5 us
    reduce_scatter x1, waiting for transfers between devices, local(): lax.psum_scatter(grads[1], 'seq', scatter_dimension=0, tiled=True)  69 us
    reduce_scatter x1, waiting for transfers between devices, local(): lax.psum_scatter(grads[3], 'seq', scatter_dimension=0, tiled=True)  67.4 us
    reduce_scatter x1, waiting for transfers between devices, local(): lax.psum_scatter(grads[2], 'seq', scatter_dimension=0, tiled=True)  66.6 us
    unnamed x456, local copies, waits for them, and re-layouts  58.6 us
  transfers between devices with their start and end apart: 53, of which 38 were waited for; matrix products, arithmetic and copies ran while one was open for 25% of the time, Pallas kernels for 0%

commit v1 on v0

v1 whole, which is shorter than its diff:
```python
import functools

import jax
import jax.numpy as jnp
from jax import lax
from jax.experimental import pallas as pl
from jax.experimental.pallas import tpu as pltpu
from jax.sharding import PartitionSpec as P

H = 12
EPSILON = 1e-06
NEGATIVE = -1e30
F32 = jnp.float32
BF = jnp.bfloat16
VM = pl.BlockSpec(memory_space=pltpu.VMEM)
SM = pl.BlockSpec(memory_space=pltpu.SMEM)
ROWS = 512
QB = 256


def dot(a, b):
    return lax.dot_general(a, b, (((1,), (0,)), ((), ())), preferred_element_type=F32)


def nt(a, b):
    return lax.dot_general(a, b, (((1,), (1,)), ((), ())), preferred_element_type=F32)


def lanes(width):
    return lax.broadcasted_iota(jnp.int32, (1, width), 1)


def inv_rms(v):
    return lax.rsqrt(jnp.mean(v * v, axis=-1, keepdims=True) + EPSILON)


def norm_back(e, v, gain):
    r = inv_rms(v)
    u = v * r
    eg = e * gain
    grad_v = (eg - u * jnp.mean(eg * u, axis=-1, keepdims=True)) * r
    return grad_v, jnp.sum(e * u, axis=0, keepdims=True)


def cost(flops, *arrays):
    total = sum(a.size * a.dtype.itemsize for a in arrays)
    return pl.CostEstimate(flops=int(flops), bytes_accessed=int(total), transcendentals=0)


def sds(shape, dtype):
    return jax.ShapeDtypeStruct(shape, dtype)


def project_kernel(
    charts, tokens, patches, meta, own, oth, gain, wq, wk, wv, ck, cv,
    x_nat, x_own, a1, q, k, v, mem, mk, mv, mem_scr,
):
    core, place = meta[0], meta[1]
    half = q.shape[1]
    width = a1.shape[1]
    group = max(1, min(charts, ROWS // tokens))
    cols = pl.ds(pl.multiple_of(core * half, 128), half)

    def one(ref, parity, first):
        x = ref[pl.ds(first, group), :tokens, :].reshape(group * tokens, width)
        xf = x.astype(F32)
        a = (xf * inv_rms(xf) * gain[...]).astype(BF)
        qq = (dot(a, wq[:, cols]) * 0.125).astype(BF)
        kk = dot(a, wk[:, cols]).astype(BF)
        vv = dot(a, wv[:, cols]).astype(BF)
        for i in range(group):
            chunk = lax.rem(place - (first + i) + charts, charts)
            part = slice(i * tokens, (i + 1) * tokens)
            at = pl.ds(pl.multiple_of((2 * chunk + parity) * tokens, tokens), tokens)
            x_nat[at, :] = x[part]
            a1[at, :] = a[part]
            q[at, :] = qq[part]
            k[at, :] = kk[part]
            v[at, :] = vv[part]
            few = ref[first + i, tokens:, :].astype(F32)
            spot = pl.ds(pl.multiple_of((2 * chunk + parity) * patches, patches), patches)
            mem_scr[spot, :] = few
            if ref is own:
                x_own[pl.ds(pl.multiple_of(chunk * tokens, tokens), tokens), :] = x[part]

    for ref, parity in ((own, core), (oth, 1 - core)):
        if charts == group:
            one(ref, parity, 0)
        else:
            lax.fori_loop(
                0, charts // group, lambda g, c, r=ref, p=parity: (one(r, p, g * group), c)[1], 0
            )
    whole = mem_scr[...].astype(BF)
    mem[...] = whole
    mk[...] = dot(whole, ck[...]).astype(BF)
    mv[...] = dot(whole, cv[...]).astype(BF)


def split3(value):
    hi = value.astype(BF).astype(F32)
    mid = (value - hi).astype(BF).astype(F32)
    lo = (value - hi - mid).astype(BF).astype(F32)
    return hi, mid, lo


def head_masks(h):
    lane = lanes(128)
    mine = ((lane < 64) if h == 0 else (lane >= 64)).astype(F32)
    base = 64 if h == 0 else 0
    marks = [(lane == base + i).astype(F32) for i in range(3)]
    return mine, marks


def add_marks(mine, marks, body, extra):
    hi, mid, lo = split3(extra)
    return (body * mine + hi * marks[0] + mid * marks[1] + lo * marks[2]).astype(BF)


def attend_kernel(tokens, meta, q, k, v, o_keep, o_send, o_nat, q_aug):
    core = meta[0]
    size = q.shape[0]
    row = lax.broadcasted_iota(jnp.int32, (QB, QB), 0)
    col = lax.broadcasted_iota(jnp.int32, (QB, QB), 1)

    def one_block(i, count):
        at = pl.ds(i * QB, QB) if count is not None else pl.ds(pl.multiple_of(i * QB, QB), QB)
        qp = q[at, :]
        outs = []
        for h in (0, 1):
            mine, marks = head_masks(h)
            mb = mine.astype(BF)
            rest = (1.0 - mine).astype(BF)
            qh = qp * mb

            def scores(j):
                return nt(qh, k[pl.ds(pl.multiple_of(j * QB, QB), QB), :])

            def weigh(e, j):
                vh = v[pl.ds(pl.multiple_of(j * QB, QB), QB), :] * mb + rest
                return dot(e.astype(BF), vh)

            diag = jnp.where(row >= col, scores(i), NEGATIVE)
            if count is not None:
                parts = [scores(j) for j in range(count - 1)] + [diag]
                top = parts[0]
                for s in parts[1:]:
                    top = jnp.maximum(top, s)
                top = jnp.max(top, axis=1, keepdims=True)
                acc = weigh(jnp.exp(parts[0] - top), 0)
                for j, s in enumerate(parts[1:]):
                    acc = acc + weigh(jnp.exp(s - top), j + 1)
            else:
                top = jnp.max(diag, axis=1, keepdims=True)
                acc = weigh(jnp.exp(diag - top), i)

                def step(j, state):
                    top, acc = state
                    s = scores(j)
                    new = jnp.maximum(top, jnp.max(s, axis=1, keepdims=True))
                    return new, acc * jnp.exp(top - new) + weigh(jnp.exp(s - new), j)

                top, acc = lax.fori_loop(0, i, step, (top, acc))
            total = pltpu.roll(acc, 64, 1)
            outs.append(acc / (total * mine + (1.0 - mine)) * mine)
            lse = top + jnp.log(acc * (1.0 - mine) + mine)
            q_aug[h, at, :] = add_marks(mine, marks, qp.astype(F32), -lse)
        o = (outs[0] + outs[1]).astype(BF)
        o_nat[at, :] = o
        per = QB // (2 * tokens)
        for c in range(per):
            even = o[2 * c * tokens : (2 * c + 1) * tokens]
            odd = o[(2 * c + 1) * tokens : (2 * c + 2) * tokens]
            spot = pl.ds(pl.multiple_of((i * per + c) * tokens, tokens), tokens)
            flag = jnp.full(even.shape, core, jnp.int32).astype(F32)
            ef, of = even.astype(F32), odd.astype(F32)
            o_keep[spot, :] = jnp.where(flag == 0, ef, of).astype(BF)
            o_send[spot, :] = jnp.where(flag == 0, of, ef).astype(BF)

    if size <= 1024:
        for i in range(size // QB):
            one_block(i, i + 1)
    else:
        lax.fori_loop(0, size // QB, lambda i, c: (one_block(i, None), c)[1], 0)


def attend_back_kernel(
    tokens, meta, q_aug, k, v, o_nat, do_own, do_oth, dq, dk, dv, k_aug, v_aug, kt, dk_acc, dv_acc
):
    core = meta[0]
    size = k.shape[0]
    krow = lax.broadcasted_iota(jnp.int32, (QB, QB), 0)
    qcol = lax.broadcasted_iota(jnp.int32, (QB, QB), 1)
    kt[...] = k[...].astype(F32).T.astype(BF)
    for h in (0, 1):
        mine, marks = head_masks(h)
        ones = (marks[0] + marks[1] + marks[2]).astype(BF)
        k_aug[h] = k[...] * mine.astype(BF) + ones
        v_aug[h] = v[...] * mine.astype(BF) + ones
    dk_acc[...] = jnp.zeros_like(dk_acc)
    dv_acc[...] = jnp.zeros_like(dv_acc)

    def one_block(i, count):
        at = pl.ds(pl.multiple_of(i * QB, QB), QB)
        per = QB // (2 * tokens)
        pieces = []
        for c in range(per):
            spot = pl.ds(pl.multiple_of((i * per + c) * tokens, tokens), tokens)
            a, b = do_own[spot, :].astype(F32), do_oth[spot, :].astype(F32)
            flag = jnp.full(a.shape, core, jnp.int32)
            pieces += [jnp.where(flag == 0, a, b), jnp.where(flag == 0, b, a)]
        do = jnp.concatenate(pieces, 0)
        prod = do * o_nat[at, :].astype(F32)
        turned = []
        for h in (0, 1):
            mine, marks = head_masks(h)
            delta = jnp.sum(prod * mine, axis=1, keepdims=True)
            doa = add_marks(mine, marks, do, -delta)
            qa = q_aug[h, at, :]

            def one(j, dqt, diagonal):
                kat = pl.ds(pl.multiple_of(j * QB, QB), QB)
                s = nt(k_aug[h, kat, :], qa)
                if diagonal:
                    s = jnp.where(qcol >= krow, s, NEGATIVE)
                p = jnp.exp(s)
                ds = (p * nt(v_aug[h, kat, :], doa)).astype(BF)
                dv_acc[h, kat, :] += dot(p.astype(BF), doa)
                dk_acc[h, kat, :] += dot(ds, qa)
                return dqt + dot(kt[64 * h : 64 * h + 64, kat], ds)

            dqt = jnp.zeros((64, QB), F32)
            if count is not None:
                for j in range(count - 1):
                    dqt = one(j, dqt, False)
            else:
                dqt = lax.fori_loop(0, i, lambda j, c: one(j, c, False), dqt)
            turned.append(one(i, dqt, True))
        dq[at, :] = (jnp.concatenate(turned, 0).T * 0.125).astype(BF)

    if size <= 1024:
        for i in range(size // QB):
            one_block(i, i + 1)
    else:
        lax.fori_loop(0, size // QB, lambda i, c: (one_block(i, None), c)[1], 0)
    m0, m1 = head_masks(0)[0], head_masks(1)[0]
    dk[...] = (dk_acc[0] * m0 + dk_acc[1] * m1).astype(BF)
    dv[...] = (dv_acc[0] * m0 + dv_acc[1] * m1).astype(BF)


def cross_pair(ref, p):
    lane = lanes(128)
    piece = ref[:, 128 * p : 128 * p + 128]
    low = (lane < 64).astype(BF)
    high = (lane >= 64).astype(BF)
    return jnp.concatenate([piece * low, piece * high], 0)


def cross_kernel(
    meta, x, o_own, o_oth, w_out, g_cross, c_query, mk, mv, c_out, g_ffn,
    o1, y1, a2, cq, p2, o2, y2, a3,
):
    core, count = meta[0], meta[2]
    half = o_own.shape[1]
    mine = pl.ds(pl.multiple_of(core * half, 128), half)
    other = pl.ds(pl.multiple_of((1 - core) * half, 128), half)
    o1[:, mine] = o_own[...]
    o1[:, other] = o_oth[...]
    first = x[...].astype(F32) + dot(o1[...], w_out[...])
    y1[...] = first
    n2 = (first * inv_rms(first) * g_cross[...]).astype(BF)
    a2[...] = n2
    query = dot(n2, c_query[...]).astype(BF)
    cq[...] = query
    patches = mk.shape[0]
    lane = lanes(2 * patches)
    low = lane < patches
    valid = jnp.where(low, lane, lane - patches) < count
    for p in range(H // 2):
        keys = cross_pair(mk, p)
        values = cross_pair(mv, p)
        s = nt(query[:, 128 * p : 128 * p + 128], keys) * 0.125
        s = jnp.where(valid, s, NEGATIVE)
        m0 = jnp.max(jnp.where(low, s, NEGATIVE), axis=1, keepdims=True)
        m1 = jnp.max(jnp.where(low, NEGATIVE, s), axis=1, keepdims=True)
        e = jnp.exp(s - jnp.where(low, m0, m1))
        l0 = jnp.sum(jnp.where(low, e, 0.0), axis=1, keepdims=True)
        l1 = jnp.sum(jnp.where(low, 0.0, e), axis=1, keepdims=True)
        w = e / jnp.where(low, l0, l1)
        p2[p] = w
        o2[:, 128 * p : 128 * p + 128] = dot(w.astype(BF), values).astype(BF)
    second = first + dot(o2[...], c_out[...])
    y2[...] = second
    a3[...] = (second * inv_rms(second) * g_ffn[...]).astype(BF)


def ffn_kernel(
    row_blocks, meta, a3, cot, y2, g_ffn, wg, wu, wd,
    out, dy2, dy2b, gain, send, keep, acc, err, a3t, cott, dw,
):
    core = meta[0]
    i, r = pl.program_id(0), pl.program_id(1)
    rows = pl.ds(pl.multiple_of(r * ROWS, ROWS), ROWS)
    first, last = i == 0, i == pl.num_programs(0) - 1

    @pl.when(first)
    def _():
        a3t[:, rows] = a3[...].astype(F32).T.astype(BF)
        cott[:, rows] = cot[...].astype(F32).T.astype(BF)
        acc[rows, :] = y2[...]
        err[rows, :] = jnp.zeros((ROWS, err.shape[1]), F32)

    gate = dot(a3[...], wg[...])
    up = dot(a3[...], wu[...])
    square = gate * gate
    th = jnp.tanh(0.7978845608028654 * gate * (1.0 + 0.044715 * square))
    more = 0.5 * (1.0 + th)
    act = gate * more
    slope = more + 0.5 * gate * (1.0 - th * th) * (
        0.7978845608028654 * (1.0 + 3 * 0.044715 * square)
    )
    hidden = (act * up).astype(BF)
    dh = nt(cot[...], wd[...])
    d_gate = (dh * up * slope).astype(BF)
    d_up = (dh * act).astype(BF)
    acc[rows, :] += dot(hidden, wd[...])
    err[rows, :] += nt(d_gate, wg[...]) + nt(d_up, wu[...])
    terms = (dot(a3t[:, rows], d_gate), dot(a3t[:, rows], d_up), dot(cott[:, rows], hidden))
    if row_blocks > 1:
        for n, term in enumerate(terms):
            dw[n] = jnp.where(r == 0, 0.0, dw[n]) + term
        terms = (dw[0], dw[1], dw[2])

    def put():
        side = i // 2
        which = lax.rem(i, 2)
        width = terms[0].shape[1]
        for n in (0, 1):
            block = terms[n].astype(BF).reshape(8, terms[n].shape[0] // 8, width)

            @pl.when(which == core)
            def _(n=n, block=block):
                keep[side, n] = block

            @pl.when(which != core)
            def _(n=n, block=block):
                send[side, n] = block

        down = terms[2].astype(BF)
        per, part, wide = down.shape[0] // 4, down.shape[0] // 8, width // 2
        for b in range(4):
            for y in range(2):
                piece = down[b * per : (b + 1) * per, y * wide : (y + 1) * wide]
                packed = jnp.concatenate([piece[:part], piece[part:]], 1)

                @pl.when(core == b % 2)
                def _(b=b, y=y, packed=packed):
                    keep[b // 2, 2, 2 * i + y] = packed

                @pl.when(core != b % 2)
                def _(b=b, y=y, packed=packed):
                    send[b // 2, 2, 2 * i + y] = packed

    if row_blocks > 1:
        pl.when(r == row_blocks - 1)(put)
    else:
        put()

    @pl.when(last)
    def _():
        out[...] = acc[rows, :].astype(BF)
        back, gsum = norm_back(err[rows, :], y2[...], g_ffn[...])
        total = cot[...].astype(F32) + back
        dy2[...] = total
        dy2b[...] = total.astype(BF)
        gain[...] = jnp.where(r == 0, 0.0, gain[...]) + gsum


def cross_back_kernel(
    charts, patches_each, meta, dy2, dy2b, c_out, p2, mk, mv, cq, y1, g_cross, c_query, w_out,
    c_key, c_value,
    dcq, dmk, dmv, dy1, dy1b, do_keep, do_send, memg, gain, mk_acc, mv_acc, mem_scr,
):
    core = meta[0]
    r = pl.program_id(0)
    half = do_keep.shape[1]
    patches = mk.shape[0]
    lane = lanes(2 * patches)
    low = lane < patches
    left = (lanes(128) < 64).astype(F32)
    do2 = nt(dy2b[...], c_out[...]).astype(BF)
    fresh = r == 0
    for p in range(H // 2):
        at = slice(128 * p, 128 * p + 128)
        keys = cross_pair(mk, p)
        values = cross_pair(mv, p)
        w = p2[p]
        dp = nt(do2[:, at], values)
        prod = w * dp
        r0 = jnp.sum(jnp.where(low, prod, 0.0), axis=1, keepdims=True)
        r1 = jnp.sum(jnp.where(low, 0.0, prod), axis=1, keepdims=True)
        ds = w * (dp - jnp.where(low, r0, r1))
        dcq[:, at] = (dot(ds.astype(BF), keys) * 0.125).astype(BF)
        gk = dot(ds.T.astype(BF), cq[:, at]) * 0.125
        gv = dot(w.T.astype(BF), do2[:, at])
        gk = gk[:patches] * left + gk[patches:] * (1.0 - left)
        gv = gv[:patches] * left + gv[patches:] * (1.0 - left)
        mk_acc[:, at] = jnp.where(fresh, 0.0, mk_acc[:, at]) + gk
        mv_acc[:, at] = jnp.where(fresh, 0.0, mv_acc[:, at]) + gv
    err = nt(dcq[...], c_query[...])
    back, gsum = norm_back(err, y1[...], g_cross[...])
    total = dy2[...] + back
    dy1[...] = total
    tb = total.astype(BF)
    dy1b[...] = tb
    gain[...] = jnp.where(fresh, 0.0, gain[...]) + gsum
    do_keep[...] = nt(tb, w_out[pl.ds(pl.multiple_of(core * half, half), half), :]).astype(BF)
    do_send[...] = nt(tb, w_out[pl.ds(pl.multiple_of((1 - core) * half, half), half), :]).astype(BF)

    @pl.when(r == pl.num_programs(0) - 1)
    def _():
        gk, gv = mk_acc[...].astype(BF), mv_acc[...].astype(BF)
        dmk[...] = gk
        dmv[...] = gv
        mem_scr[...] = nt(gk, c_key[...]) + nt(gv, c_value[...])
        for a in range(charts):
            for parity in range(2):
                memg[parity, a] = mem_scr[pl.ds((2 * a + parity) * patches_each, patches_each), :]


def square_kernel(meta, o2, dy2b, a2, dcq, mem, dmk, dmv, o1, dy1b, send, keep):
    core = meta[0]
    half = keep.shape[2]
    mine = pl.ds(pl.multiple_of(core * half, 128), half)
    other = pl.ds(pl.multiple_of((1 - core) * half, 128), half)
    memt = mem[...].astype(F32).T.astype(BF)
    pairs = ((o2, dy2b), (a2, dcq), (None, dmk), (None, dmv), (o1, dy1b))
    for n, (left, right) in enumerate(pairs):
        turned = memt if left is None else left[...].astype(F32).T.astype(BF)
        send[n] = dot(turned, right[:, other]).astype(BF)
        keep[n] = dot(turned, right[:, mine]).astype(BF)


def entry_kernel(charts, tokens, meta, dq, dk, dv, wq, wk, wv, x_nat, e_keep, e_send, gain, scr):
    core = meta[0]
    half = dq.shape[1]
    cols = pl.ds(pl.multiple_of(core * half, 128), half)
    size = dq.shape[0]
    step = min(size, 2 * ROWS)
    gain[...] = jnp.zeros_like(gain)
    per = step // (2 * tokens)

    def one(first):
        at = pl.ds(pl.multiple_of(first * step, step), step)
        e = nt(dq[at, :], wq[:, cols]) + nt(dk[at, :], wk[:, cols]) + nt(dv[at, :], wv[:, cols])
        scr[...] = e
        x = x_nat[at, :].astype(F32)
        gain[...] += jnp.sum(e * (x * inv_rms(x)), axis=0, keepdims=True)
        for c in range(per):
            spot = pl.ds(pl.multiple_of((first * per + c) * tokens, tokens), tokens)
            e_keep[spot, :] = scr[pl.ds(pl.multiple_of((2 * c + core) * tokens, tokens), tokens), :]
            e_send[spot, :] = scr[
                pl.ds(pl.multiple_of((2 * c + 1 - core) * tokens, tokens), tokens), :
            ].astype(BF)

    if size == step:
        one(0)
    else:
        lax.fori_loop(0, size // step, lambda g, c: (one(g), c)[1], 0)


def triple_kernel(a1, dq, dk, dv, g_self, g_cross, g_ffn, out):
    half = dq.shape[1]
    turned = a1[...].astype(F32).T.astype(BF)
    for n, right in enumerate((dq, dk, dv)):
        out[:, n * half : (n + 1) * half] = dot(turned, right[...]).astype(BF)
    width = g_self.shape[1]
    stack = jnp.concatenate(
        [g_self[...], g_cross[...], g_ffn[...], jnp.zeros((125, width), F32)], 0
    )
    out[:, 3 * half :] = stack.T.astype(BF)


def input_grad_kernel(e_keep, e_recv, x, gain, dy1, out):
    err = e_keep[...] + e_recv[...].astype(F32)
    back, _ = norm_back(err, x[...].astype(F32), gain[...])
    out[...] = (dy1[...] + back).astype(BF)


def place_kernel(charts, meta, *refs):
    place = meta[1]
    out = refs[-1]
    for d in range(charts):
        out[lax.rem(place - d + charts, charts)] = refs[d][...].astype(F32)


def local(
    nseq, inputs, memory, patch_count, cotangent, norm_self, w_query, w_key, w_value, w_out,
    norm_cross, c_query, c_key, c_value, c_out, norm_ffn, w_gate, w_up, w_down,
):
    charts, tokens, width = inputs.shape
    patches_each = memory.shape[1]
    size = charts * 2 * tokens
    own = charts * tokens
    patches = patches_each * nseq
    half = width // 2
    hidden = w_gate.shape[1]
    blocks = own // ROWS
    dp = lax.axis_index("dp")
    seq = lax.axis_index("seq")
    side, core = dp // 2, lax.rem(dp, 2)
    place, parity = seq // 2, lax.rem(seq, 2)

    def shift(d):
        return [
            ((2 * x + k) * nseq + 2 * a + b, (2 * x + b) * nseq + 2 * ((a + d) % charts) + k)
            for x in range(2)
            for k in range(2)
            for a in range(charts)
            for b in range(2)
        ]

    def dp_perm(rule):
        return [(2 * x + k, 2 * rule(x, k)[0] + rule(x, k)[1]) for x in range(2) for k in range(2)]

    swap_core = dp_perm(lambda x, k: (x, 1 - k))
    swap_side = dp_perm(lambda x, k: (1 - x, k))

    def across(value):
        return lax.ppermute(value, "dp", swap_core)

    def travel(value, d):
        return lax.ppermute(value, ("dp", "seq"), shift(d))

    def pick(value, d):
        return lax.dynamic_index_in_dim(value, lax.rem(place + d, charts), 0, keepdims=False)

    gain_self, gain_cross, gain_ffn = (g.reshape(1, width) for g in (norm_self, norm_cross, norm_ffn))
    other_counts = across(patch_count)
    counts = jnp.where(core == parity, patch_count, other_counts)
    count = lax.dynamic_index_in_dim(counts, place, 0, keepdims=False)
    meta = jnp.stack([core, place, count, side]).astype(jnp.int32)

    mine = jnp.stack(
        [
            travel(jnp.concatenate([pick(inputs, d), pick(memory, d)], 0), d)
            for d in range(charts)
        ]
    )
    theirs = across(mine)
    x_nat, x_own, a1, q, k, v, mem, mk, mv = pl.pallas_call(
        functools.partial(project_kernel, charts, tokens, patches_each),
        out_shape=(
            sds((size, width), BF), sds((own, width), BF), sds((size, width), BF),
            sds((size, half), BF), sds((size, half), BF), sds((size, half), BF),
            sds((patches, width), BF), sds((patches, width), BF), sds((patches, width), BF),
        ),
        in_specs=[SM] + [VM] * 8,
        out_specs=[VM] * 9,
        scratch_shapes=[pltpu.VMEM((patches, width), F32)],
        cost_estimate=cost(2 * size * width * 3 * half, mine, theirs, w_query, w_key, w_value),
    )(meta, mine, theirs, gain_self, w_query, w_key, w_value, c_key, c_value)

    cot_parts = [travel(pick(cotangent, d), d) for d in range(charts)]

    pairs = half // 128
    pair_spec = pl.BlockSpec((size, 128), lambda p, m: (0, p))
    own_spec = pl.BlockSpec((own, 128), lambda p, m: (0, p))
    aug_spec = pl.BlockSpec((2, size, 128), lambda p, m: (p, 0, 0))
    o_keep, o_send, o_nat, q_aug = pl.pallas_call(
        functools.partial(attend_kernel, tokens),
        out_shape=(
            sds((own, half), BF), sds((own, half), BF), sds((size, half), BF),
            sds((2 * pairs, size, 128), BF),
        ),
        grid_spec=pltpu.PrefetchScalarGridSpec(
            num_scalar_prefetch=1,
            grid=(pairs,),
            in_specs=[pair_spec] * 3,
            out_specs=[own_spec, own_spec, pair_spec, aug_spec],
        ),
        cost_estimate=cost(4 * size * size * half, q, k, v),
    )(meta, q, k, v)
    o_recv = across(o_send)

    row_spec = pl.BlockSpec((ROWS, width), lambda r: (r, 0))
    half_spec = pl.BlockSpec((ROWS, half), lambda r: (r, 0))
    p2_spec = pl.BlockSpec((H // 2, ROWS, 2 * patches), lambda r: (0, r, 0))

    def fixed(shape, spaces=1):
        if spaces == 1:
            return pl.BlockSpec(shape, lambda r: (0,) * len(shape))
        return pl.BlockSpec(shape, lambda i, r: (0,) * len(shape))

    square = fixed((width, width))
    one_row = fixed((1, width))
    patch_spec = fixed((patches, width))
    rows_f = sds((own, width), F32)
    rows_b = sds((own, width), BF)
    o1, y1, a2, cq, p2, o2, y2, a3 = pl.pallas_call(
        cross_kernel,
        out_shape=(
            rows_b, rows_f, rows_b, rows_b, sds((H // 2, own, 2 * patches), F32), rows_b, rows_f,
            rows_b,
        ),
        grid=(blocks,),
        in_specs=[
            SM, row_spec, half_spec, half_spec, square, one_row, square, patch_spec, patch_spec,
            square, one_row,
        ],
        out_specs=[row_spec] * 4 + [p2_spec] + [row_spec] * 3,
        cost_estimate=cost(6 * own * width * width, w_out, c_query, c_out, rows_f, rows_f),
    )(meta, x_own, o_keep, o_recv, w_out, gain_cross, c_query, mk, mv, c_out, gain_ffn)

    cot = lax.dynamic_slice_in_dim(
        jnp.concatenate(cot_parts[::-1] + cot_parts[::-1], 0),
        (charts - 1 - place) * tokens,
        own,
        0,
    )
    wide = hidden // 4
    last = 3
    pack = (2, 3, 8, width // 8, wide)
    frow = pl.BlockSpec((ROWS, width), lambda i, r: (r, 0))
    lrow = pl.BlockSpec((ROWS, width), lambda i, r: (r * (i // last), 0))
    out_b, dy2, dy2b, ffn_gain, f_send, f_keep = pl.pallas_call(
        functools.partial(ffn_kernel, blocks),
        out_shape=(rows_b, rows_f, rows_b, sds((1, width), F32), sds(pack, BF), sds(pack, BF)),
        grid=(4, blocks),
        in_specs=[
            SM, frow, frow, frow, fixed((1, width), 2),
            pl.BlockSpec((width, wide), lambda i, r: (0, i)),
            pl.BlockSpec((width, wide), lambda i, r: (0, i)),
            pl.BlockSpec((wide, width), lambda i, r: (i, 0)),
        ],
        out_specs=[lrow, lrow, lrow, fixed((1, width), 2), fixed(pack, 2), fixed(pack, 2)],
        scratch_shapes=[
            pltpu.VMEM((own, width), F32), pltpu.VMEM((own, width), F32),
            pltpu.VMEM((width, own), BF), pltpu.VMEM((width, own), BF),
            pltpu.VMEM((3, width, wide) if blocks > 1 else (3, 8, 128), F32),
        ],
        cost_estimate=cost(18 * own * width * hidden, w_gate, w_up, w_down, rows_f, rows_f),
    )(meta, a3, cot, y2, gain_ffn, w_gate, w_up, w_down)
    f_recv = across(f_send)

    dcq, dmk, dmv, dy1, dy1b, do_keep, do_send, memg, cross_gain = pl.pallas_call(
        functools.partial(cross_back_kernel, charts, patches_each),
        out_shape=(
            rows_b, sds((patches, width), BF), sds((patches, width), BF), rows_f, rows_b,
            sds((own, half), BF), sds((own, half), BF),
            sds((2, charts, patches_each, width), F32), sds((1, width), F32),
        ),
        grid=(blocks,),
        in_specs=[
            SM, row_spec, row_spec, square, p2_spec, patch_spec, patch_spec, row_spec, row_spec,
            one_row, square, square, square, square,
        ],
        out_specs=[
            row_spec, patch_spec, patch_spec, row_spec, row_spec, half_spec, half_spec,
            fixed((2, charts, patches_each, width)), one_row,
        ],
        scratch_shapes=[pltpu.VMEM((patches, width), F32)] * 3,
        cost_estimate=cost(6 * own * width * width, w_out, c_query, c_out, rows_f, rows_f),
    )(meta, dy2, dy2b, c_out, p2, mk, mv, cq, y1, gain_cross, c_query, w_out, c_key, c_value)
    do_recv = across(do_send)

    s_send, s_keep = pl.pallas_call(
        square_kernel,
        out_shape=(sds((5, width, half), BF), sds((5, width, half), BF)),
        in_specs=[SM] + [VM] * 9,
        out_specs=[VM] * 2,
        cost_estimate=cost(6 * own * width * width, o1, o2, a2, dcq, dy2b, dy1b),
    )(meta, o2, dy2b, a2, dcq, mem, dmk, dmv, o1, dy1b)
    s_recv = across(s_send)

    memg_send = lax.dynamic_index_in_dim(memg, 1 - core, 0, keepdims=False).astype(BF)
    memg_keep = lax.dynamic_index_in_dim(memg, core, 0, keepdims=False)
    memg_own = (memg_keep + across(memg_send).astype(F32)).astype(BF)
    out_rows = jnp.concatenate([out_b.reshape(charts, tokens, width), memg_own], 1)
    out_parts = [travel(pick(out_rows, d), d) for d in range(charts)]

    dq, dk, dv = pl.pallas_call(
        functools.partial(attend_back_kernel, tokens),
        out_shape=(sds((size, half), BF),) * 3,
        grid_spec=pltpu.PrefetchScalarGridSpec(
            num_scalar_prefetch=1,
            grid=(pairs,),
            in_specs=[aug_spec, pair_spec, pair_spec, pair_spec, own_spec, own_spec],
            out_specs=[pair_spec] * 3,
            scratch_shapes=[
                pltpu.VMEM((2, size, 128), BF), pltpu.VMEM((2, size, 128), BF),
                pltpu.VMEM((128, size), BF),
                pltpu.VMEM((2, size, 128), F32), pltpu.VMEM((2, size, 128), F32),
            ],
        ),
        cost_estimate=cost(10 * size * size * half, q, k, v, q_aug),
    )(meta, q_aug, k, v, o_nat, do_keep, do_recv)

    e_keep, e_send, self_gain = pl.pallas_call(
        functools.partial(entry_kernel, charts, tokens),
        out_shape=(rows_f, rows_b, sds((1, width), F32)),
        in_specs=[SM] + [VM] * 7,
        out_specs=[VM] * 3,
        scratch_shapes=[pltpu.VMEM((min(size, 2 * ROWS), width), F32)],
        cost_estimate=cost(2 * size * width * 3 * half, dq, dk, dv, rows_f),
    )(meta, dq, dk, dv, w_query, w_key, w_value, x_nat)
    e_recv = across(e_send)

    t_keep = pl.pallas_call(
        triple_kernel,
        out_shape=sds((width, 3 * half + 128), BF),
        in_specs=[VM] * 7,
        out_specs=VM,
        cost_estimate=cost(2 * size * width * 3 * half, dq, dk, dv, a1),
    )(a1, dq, dk, dv, self_gain, cross_gain, ffn_gain)

    in_grad = pl.pallas_call(
        input_grad_kernel,
        out_shape=rows_b,
        in_specs=[VM] * 5,
        out_specs=VM,
        cost_estimate=cost(20 * own * width, e_keep, e_send, x_own, dy1),
    )(e_keep, e_recv, x_own, gain_self, dy1)
    in_rows = in_grad.reshape(charts, tokens, width)
    in_parts = [travel(pick(in_rows, d), d) for d in range(charts)]

    def total(parts):
        result = parts[0].astype(F32)
        for part in parts[1:]:
            result = result + part.astype(F32)
        return result

    def halve(parts, axis, index, name, perm):
        send = total(
            [lax.dynamic_index_in_dim(p, 1 - index, axis, keepdims=False) for p in parts]
        ).astype(BF)
        kept = [lax.dynamic_index_in_dim(p, index, axis, keepdims=False) for p in parts]
        return kept + [lax.ppermute(send, name, perm)]

    f_parts = halve([f_keep, f_recv], 0, side, "dp", swap_side)
    s_parts = [s_keep, s_recv]
    if nseq == 8:
        bits = (parity, lax.rem(place, 2), place // 2)
        perms = [[(s, s ^ (1 << b)) for s in range(8)] for b in range(3)]

        def over_seq(parts, axis):
            shape = parts[0].shape
            parts = [
                p.reshape(shape[:axis] + (2, 2, 2, shape[axis] // 8) + shape[axis + 1 :])
                for p in parts
            ]
            for b in range(3):
                parts = halve(parts, axis + 2 - b, bits[b], "seq", perms[b])
            return total(parts)

        f_sum = over_seq([p.reshape(3, width, wide) for p in f_parts], 1)
        s_sum = over_seq(s_parts, 1)
        t_sum = over_seq([t_keep], 0)
        g_gate, g_up = f_sum[0], f_sum[1]
        g_down = f_sum[2].reshape(width // 8, 2, wide // 2).transpose(2, 1, 0).reshape(wide // 2, width // 4)
    else:

        def over_seq(value, axis):
            return lax.psum_scatter(
                value.astype(BF), "seq", scatter_dimension=axis, tiled=True
            ).astype(F32)

        f_all = total(f_parts)
        g_two = over_seq(f_all[:2].reshape(2, width, wide), 1)
        g_gate, g_up = g_two[0], g_two[1]
        down = f_all[2].reshape(8, width // 8, 2, wide // 2).transpose(0, 3, 2, 1)
        g_down = over_seq(down.reshape(hidden, width // 4), 0)
        s_sum = over_seq(total(s_parts), 1)
        t_sum = over_seq(t_keep, 0)

    rows = t_sum.shape[0]
    quarter = half // 2
    t_sum = t_sum.astype(BF)
    squares = jnp.concatenate(
        [t_sum[:, : 3 * half].reshape(rows, 3, half).transpose(1, 0, 2), s_sum.astype(BF)], 0
    ).reshape(8, rows, 2, quarter)
    gains = t_sum[:, 3 * half :]
    padded = jnp.pad(gains, ((0, 0), (0, quarter - 128)))[None]

    def deliver(block, rule):
        part = lax.dynamic_index_in_dim(squares, block, 2, keepdims=False)
        return lax.ppermute(jnp.concatenate([part, padded], 0), "dp", dp_perm(rule)).astype(F32)

    done = deliver(side, lambda x, k: (k, x)) + deliver(1 - side, lambda x, k: (k, 1 - x))
    rest = lax.ppermute(gains, "dp", dp_perm(lambda x, k: (1 - k, x))).astype(F32) + lax.ppermute(
        gains, "dp", dp_perm(lambda x, k: (1 - k, 1 - x))
    ).astype(F32)
    gain_sum = done[8, :, :128] + rest

    def placed(parts):
        return pl.pallas_call(
            functools.partial(place_kernel, charts),
            out_shape=sds((charts,) + parts[0].shape, F32),
            in_specs=[SM] + [VM] * charts,
            out_specs=VM,
        )(meta, *parts)

    out_all = placed(out_parts)
    return (
        out_all[:, :tokens],
        placed(in_parts),
        out_all[:, tokens:],
        gain_sum[:, 0],
        done[0],
        done[1],
        done[2],
        done[7],
        gain_sum[:, 1],
        done[4],
        done[5],
        done[6],
        done[3],
        gain_sum[:, 2],
        g_gate,
        g_up,
        g_down,
    )


def solution(mesh):
    tok = P("dp", "seq", None)
    cut = P("seq", "dp")
    in_specs = (tok, tok, P("dp"), tok) + (P(),) * 14
    out_specs = (tok, tok, tok, P("seq"), cut, cut, cut, cut, P("seq"), cut, cut, cut, cut)
    out_specs += (P("seq"), cut, cut, cut)
    return jax.shard_map(
        functools.partial(local, mesh.shape["seq"]),
        mesh=mesh,
        in_specs=in_specs,
        out_specs=out_specs,
        check_vma=False,
    )
```

time: 1730 us -> 375 us (0.22)
  waiting for transfers between devices: 896 us -> 114 us
  local copies, waits for them, and re-layouts: 308 us -> 31.2 us
  matrix products: 205 us -> 0 us
  Pallas kernels: 0 us -> 127 us
  starting transfers between devices: 157 us -> 65.8 us
  blocking collectives: 52.8 us -> 0 us
  other arithmetic: 76.1 us -> 31.4 us
    reduce_scatter x13 -> x0, waiting for transfers between devices: 598 us -> none  [the longest x1 115 us: local(): lax.psum_scatter(grads[13], 'seq', scatter_dimension=0, tiled=True)]
    dot_general x114 -> x0, matrix products: 205 us -> none  [the longest x22 45.6 us: left_product(): lax.dot_general(left, right, (((0,), (0,)), ((), ())), preferred_element_...]
    all_to_all x31 -> x0, waiting for transfers between devices: 156 us -> none  [the longest x2 26.7 us: local(): lax.all_to_all(self_dq.astype(jnp.bfloat16).reshape(items, length * head)...]
    all_to_all x31 -> x0, starting transfers between devices: 155 us -> none  [the longest x2 13.5 us: local(): lax.all_to_all(query_self, 'seq', split_axis=0, concat_axis=1, tiled=True)]
    unnamed x31 -> x0, waiting for transfers between devices: 142 us -> none
    pallas_call x0 -> x12, Pallas kernels: none -> 127 us  [the longest x1 28.7 us: local(): pl.pallas_call(functools.partial(attend_back_kernel, tokens), out_shape=(...]
    ppermute x0 -> x38, waiting for transfers between devices: none -> 114 us  [the longest x10 96.2 us: halve(): return kept + [lax.ppermute(send, name, perm)]]
    all_to_all x48 -> x0, local copies, waits for them, and re-layouts: 73 us -> none  [the longest x4 9.31 us: local(): lax.all_to_all(fetched_heads.reshape(items, length * head), 'seq', split_...]
  transfers between devices with their start and end apart: 53 -> 38, of which waited for: 38 -> 14; matrix products, arithmetic and copies ran while one was open for 25% -> 13% of each run, Pallas kernels for 0% -> 19%
where the time goes in v1:
time: 375 us; the launch traced here: 371 us
  Pallas kernels  127 us (34%)
  waiting for transfers between devices  114 us (30%)
  starting transfers between devices  65.8 us (18%)
  other arithmetic  31.4 us (8%)
  local copies, waits for them, and re-layouts  31.2 us (8%)
    ppermute x10, waiting for transfers between devices, halve(): return kept + [lax.ppermute(send, name, perm)]  96.2 us
    ppermute x16, starting transfers between devices, travel(): return lax.ppermute(value, ('dp', 'seq'), shift(d))  34.1 us
    pallas_call x1, Pallas kernels, local(): pl.pallas_call(functools.partial(attend_back_kernel, tokens), out_shape=(...  28.7 us
    pallas_call x1, Pallas kernels, local(): pl.pallas_call(functools.partial(ffn_kernel, blocks), out_shape=(rows_b,...  26.5 us
    convert_element_type x9, other arithmetic, halve(): send = total([lax.dynamic_index_in_dim(p, 1 - index, axis, keepdims=False...  21.6 us
    pallas_call x1, Pallas kernels, local(): pl.pallas_call(functools.partial(attend_kernel, tokens), out_shape=(sds((...  13 us
    pallas_call x1, Pallas kernels, local(): pl.pallas_call(functools.partial(cross_back_kernel, charts, patches_each)...  11.3 us
    ppermute x16, waiting for transfers between devices, travel(): return lax.ppermute(value, ('dp', 'seq'), shift(d))  11.2 us
  transfers between devices with their start and end apart: 38, of which 14 were waited for; matrix products, arithmetic and copies ran while one was open for 13% of the time, Pallas kernels for 19%

profile of v1, /device:TPU:0, one launch (start us, length us, event | category | flops | bytes accessed | tf_op | source)
XLA Modules:
  0.0 370.6 jit_solution(1299489784317147578)
XLA Ops:
  2.9 5.1 %collective-permute-start.4 = (bf16[136,768]{1,0:T(8,128)(2,1)S(1)}, bf16[136,768]{1,0:T(8,128)(2,1)S(1)}, u32[]{:S(2)}, u32[]{:S(2)}) collective-permute-start(bf16[136,768]{1,0:T(8,128)(2,1)S(1)} %pad_maximum_fusion.7), channel_id=1, source_target_pairs={{0,6},{1,14},{2,0},{3,8},{4,2},{5,10},{6,4},{7,12},{8,7},{9,15},{1... | collective-permute-start | bytes 626696 | tf_op jit(solution)/shard_map/ppermute | solution.py:532
  18.2 8.5 %collective-permute-done.3 = bf16[136,768]{1,0:T(8,128)(2,1)S(1)} collective-permute-done((bf16[136,768]{1,0:T(8,128)(2,1)S(1)}, bf16[136,768]{1,0:T(8,128)(2,1)S(1)}, u32[]{:S(2)}, u32[]{:S(2)}) %collective-permute-start.3) | collective-permute-done | bytes 208928 | tf_op jit(solution)/shard_map/ppermute | solution.py:532
  26.7 9.9 %collective-permute-start.9 = (bf16[128,768]{1,0:T(8,128)(2,1)S(1)}, bf16[128,768]{1,0:T(8,128)(2,1)S(1)}, u32[]{:S(2)}, u32[]{:S(2)}) collective-permute-start(bf16[128,768]{1,0:T(8,128)(2,1)S(1)} %get-tuple-element.129), channel_id=1, source_target_pairs={{0,2},{1,10},{2,4},{3,12},{4,6},{5,14},{6,0},{7,8},{8,3},{9,11},{1... | collective-permute-start | bytes 589832 | tf_op jit(solution)/shard_map/ppermute | solution.py:532
  45.7 8.8 %shard_map.305 = (bf16[1024,768]{1,0:T(8,128)(2,1)}, bf16[512,768]{1,0:T(8,128)(2,1)}, bf16[1024,768]{1,0:T(8,128)(2,1)}, bf16[1024,384]{1,0:T(8,128)(2,1)}, bf1...) custom-call(s32[4]{0:T(128)} %pad_add_fusion.meta, ...), custom_call_target="tpu_custom_call" | custom-call | flops 1811939328 | bytes 5210112 | tf_op jit(solution)/shard_map/pallas_call | solution.py:550
  54.5 13.0 %shard_map.306 = (bf16[512,384]{1,0:T(8,128)(2,1)}, bf16[512,384]{1,0:T(8,128)(2,1)}, bf16[1024,384]{1,0:T(8,128)(2,1)}, bf16[6,1024,128]{2,1,0:T(8,128)(2,1)}) custom-call(s32[4]{0:T(128)} %pad_add_fusion.meta, bf16[1024,384]{1,0:T(8,128)(2,1)} %get-tuple-element.62.q, bf16[1024,384]{1,0:T(8,128)(2,1)} %get-tuple-element.63.k, ...), custom_call_target="tpu_custom_call" | custom-call | flops 1610612736 | bytes 2359296 | tf_op jit(solution)/shard_map/pallas_call | solution.py:569
  71.4 8.1 %shard_map.307 = (bf16[512,768]{1,0:T(8,128)(2,1)}, f32[512,768]{1,0:T(8,128)}, bf16[512,768]{1,0:T(8,128)(2,1)}, bf16[512,768]{1,0:T(8,128)(2,1)}, f32[6,512,12...) custom-call(s32[4]{0:T(128)} %pad_add_fusion.meta, ...), custom_call_target="tpu_custom_call" | custom-call | flops 1811939328 | bytes 6684672 | tf_op jit(solution)/shard_map/pallas_call | solution.py:599
  79.5 26.5 %shard_map.308 = (bf16[512,768]{1,0:T(8,128)(2,1)}, f32[512,768]{1,0:T(8,128)}, bf16[512,768]{1,0:T(8,128)(2,1)}, f32[1,768]{1,0:T(1,128)}, bf16[2,3,8,96,512]{4...) custom-call(s32[4]{0:T(128)} %pad_add_fusion.meta, bf16[512,768]{1,0:T(8,128)(2,1)} %get-tuple-element.69.a3, ...), custom_call_target="tpu_custom_call" | custom-call | flops 14495514624 | bytes 12582912 | tf_op jit(solution)/shard_map/pallas_call | solution.py:625
  106.5 11.3 %shard_map.309 = (bf16[512,768]{1,0:T(8,128)(2,1)}, bf16[64,768]{1,0:T(8,128)(2,1)}, bf16[64,768]{1,0:T(8,128)(2,1)}, f32[512,768]{1,0:T(8,128)}, bf16[512,768]{...) custom-call(s32[4]{0:T(128)} %pad_add_fusion.meta, ...), custom_call_target="tpu_custom_call" | custom-call | flops 1811939328 | bytes 6684672 | tf_op jit(solution)/shard_map/pallas_call | solution.py:645
  117.8 7.8 %shard_map.316 = (bf16[5,768,384]{2,1,0:T(8,128)(2,1)}, bf16[5,768,384]{2,1,0:T(8,128)(2,1)}) custom-call(s32[4]{0:T(128)} %pad_add_fusion.meta, bf16[512,768]{1,0:T(8,128)(2,1)} %get-tuple-element.93.o2, bf16[512,768]{1,0:T(8,128)(2,1)} %get-tuple-element.73.dy2b, bf16[512,768]{1,0:T(8,128)(2,1)} %get-tuple-element.94.a2, ...), custom_call_target="tpu_custom_call" | custom-call | flops 1811939328 | bytes 4718592 | tf_op jit(solution)/shard_map/pallas_call | solution.py:666
  126.2 5.2 %collective-permute-done.16.do_oth = bf16[512,384]{1,0:T(8,128)(2,1)S(1)} collective-permute-done((bf16[512,384]{1,0:T(8,128)(2,1)S(1)}, bf16[512,384]{1,0:T(8,128)(2,1)S(1)}, u32[]{:S(2)}, u32[]{:S(2)}) %collective-permute-start.16) | collective-permute-done | bytes 393248 | tf_op jit(solution)/shard_map/ppermute | solution.py:529
  132.1 28.7 %shard_map.311 = (bf16[1024,384]{1,0:T(8,128)(2,1)}, bf16[1024,384]{1,0:T(8,128)(2,1)}, bf16[1024,384]{1,0:T(8,128)(2,1)}) custom-call(s32[4]{0:T(128)} %pad_add_fusion.meta, bf16[6,1024,128]{2,1,0:T(8,128)(2,1)} %get-tuple-element.78.q_aug, bf16[1024,384]{1,0:T(8,128)(2,1)} %get-tuple-element.63.k, bf16[1024,384]{1,0:T(8,128)(2,1)} %get-tuple-element.64.v, ...), custom_call_target="tpu_custom_call" | custom-call | flops 4026531840 | bytes 3932160 | tf_op jit(solution)/shard_map/pallas_call | solution.py:681
  160.8 7.5 %shard_map.312 = (f32[512,768]{1,0:T(8,128)}, bf16[512,768]{1,0:T(8,128)(2,1)}, f32[1,768]{1,0:T(1,128)}) custom-call(s32[4]{0:T(128)} %pad_add_fusion.meta, bf16[1024,384]{1,0:T(8,128)(2,1)} %get-tuple-element.82.dq, bf16[1024,384]{1,0:T(8,128)(2,1)} %get-tuple-element.83.dk, bf16[1024,384]{1,0:T(8,128)(2,1)} %get-tuple-element.84.dv, bf16[768,768]{1,0:T(8,128)(2,1)} %wq.3, ...), custom_call_target="tpu_custom_call" | custom-call | flops 1811939328 | bytes 3932160 | tf_op jit(solution)/shard_map/pallas_call | solution.py:698
  168.3 6.2 %shard_map.315 = bf16[768,1280]{1,0:T(8,128)(2,1)} custom-call(bf16[1024,768]{1,0:T(8,128)(2,1)} %get-tuple-element.89.a1, bf16[1024,384]{1,0:T(8,128)(2,1)} %get-tuple-element.82.dq, bf16[1024,384]{1,0:T(8,128)(2,1)} %get-tuple-element.83.dk, bf16[1024,384]{1,0:T(8,128)(2,1)} %get-tuple-element.84.dv, f32[1,768]{1,0:T(1,128)} %get-tuple-element.90.g_self, ...), custom_call_target="tpu_custom_call" | custom-call | flops 1811939328 | bytes 3932160 | tf_op jit(solution)/shard_map/pallas_call | solution.py:708
  180.6 4.7 %fusion = bf16[3,8,96,512]{3,2,1,0:T(8,128)(2,1)} fusion(bf16[2,3,8,96,512]{4,3,2,1,0:T(8,128)(2,1)} %collective-permute-done.33, s32[]{:T(128)S(6)} %select_n.186, bf16[2,3,8,96,512]{4,3,2,1,0:T(8,128)(2,1)} %get-tuple-element.103), kind=kLoop, calls=%fused_computation.2 | loop fusion | flops 4718592 | bytes 7077892 | tf_op jit(solution)/shard_map/convert_element_type | solution.py:735
  189.3 44.1 %collective-permute-done.22 = bf16[2,2,96,1280]{3,2,1,0:T(8,128)(2,1)S(1)} collective-permute-done((bf16[2,2,96,1280]{3,2,1,0:T(8,128)(2,1)}, bf16[2,2,96,1280]{3,2,1,0:T(8,128)(2,1)S(1)}, u32[]{:S(2)}, u32[]{:S(2)}) %collective-permute-start.22) | collective-permute-done | bytes 983072 | tf_op jit(solution)/shard_map/ppermute | solution.py:737
  241.0 3.4 collective-permute-start.12
  246.3 4.0 %shard_map.313 = bf16[512,768]{1,0:T(8,128)(2,1)} custom-call(f32[512,768]{1,0:T(8,128)} %get-tuple-element.86.e_keep, bf16[512,768]{1,0:T(8,128)(2,1)} %collective-permute-done.17.e_recv, bf16[512,768]{1,0:T(8,128)(2,1)} %get-tuple-element.61.x, f32[1,768]{1,0:T(1,128)} %reshape.204.gain, f32[512,768]{1,0:T(8,128)} %get-tuple-element.88.dy1), custom_call_target="tpu_custom_call" | custom-call | flops 7864320 | bytes 4718592 | tf_op jit(solution)/shard_map/pallas_call | solution.py:716
  258.3 15.0 %collective-permute-done.27 = bf16[5,2,96,384]{3,2,0,1:T(8,128)(2,1)} collective-permute-done((bf16[5,2,96,384]{3,2,0,1:T(8,128)(2,1)}, bf16[5,2,96,384]{3,2,0,1:T(8,128)(2,1)}, u32[]{:S(2)}, u32[]{:S(2)}) %collective-permute-start.27) | collective-permute-done | bytes 737312 | tf_op jit(solution)/shard_map/ppermute | solution.py:737
  281.3 12.2 %collective-permute-done.24 = bf16[96,1280]{1,0:T(8,128)(2,1)S(1)} collective-permute-done((bf16[96,1280]{1,0:T(8,128)(2,1)S(1)}, bf16[96,1280]{1,0:T(8,128)(2,1)S(1)}, u32[]{:S(2)}, u32[]{:S(2)}) %collective-permute-start.24) | collective-permute-done | bytes 245792 | tf_op jit(solution)/shard_map/ppermute | solution.py:737
  295.9 5.5 %collective-permute-done.28 = bf16[5,96,384]{2,1,0:T(8,128)(2,1)} collective-permute-done((bf16[5,96,384]{2,1,0:T(8,128)(2,1)}, bf16[5,96,384]{2,1,0:T(8,128)(2,1)}, u32[]{:S(2)}, u32[]{:S(2)}) %collective-permute-start.28) | collective-permute-done | bytes 368672 | tf_op jit(solution)/shard_map/ppermute | solution.py:737
  315.4 5.0 %collective-permute-start.29 = (bf16[9,96,192]{2,1,0:T(8,128)(2,1)}, bf16[9,96,192]{2,1,0:T(8,128)(2,1)}, u32[]{:S(2)}, u32[]{:S(2)}) collective-permute-start(bf16[9,96,192]{2,1,0:T(8,128)(2,1)} %get-tuple-element.137), channel_id=1, source_target_pairs={{0,0},{8,16},{16,8},{24,24},{1,1},{9,17},{17,9},{25,25},{2,2},{10,... | collective-permute-start | bytes 995336 | tf_op jit(solution)/shard_map/ppermute | solution.py:786
  323.8 3.9 %collective-permute-start.21 = (bf16[128,768]{1,0:T(8,128)(2,1)}, bf16[128,768]{1,0:T(8,128)(2,1)}, u32[]{:S(2)}, u32[]{:S(2)}) collective-permute-start(bf16[128,768]{1,0:T(8,128)(2,1)} %get-tuple-element.122), channel_id=1, source_target_pairs={{0,6},{1,14},{2,0},{3,8},{4,2},{5,10},{6,4},{7,12},{8,7},{9,15},{1... | collective-permute-start | bytes 589832 | tf_op jit(solution)/shard_map/ppermute | solution.py:532
  340.3 5.8 %collective-permute-start.32 = (bf16[96,128]{1,0:T(8,128)(2,1)}, bf16[96,128]{1,0:T(8,128)(2,1)S(1)}, u32[]{:S(2)}, u32[]{:S(2)}) collective-permute-start(bf16[96,128]{1,0:T(8,128)(2,1)} %copy-done.14), channel_id=1, source_target_pairs={{0,24},{8,8},{16,16},{24,0},{1,25},{9,9},{17,17},{25,1},{2,26},{10... | collective-permute-start | bytes 73736 | tf_op jit(solution)/shard_map/ppermute | solution.py:789
  352.6 14.8 %collective-permute-done.37 = bf16[3,96,512]{2,1,0:T(8,128)(2,1)S(1)} collective-permute-done((bf16[3,96,512]{2,1,0:T(8,128)(2,1)S(1)}, bf16[3,96,512]{2,1,0:T(8,128)(2,1)S(1)}, u32[]{:S(2)}, u32[]{:S(2)}) %collective-permute-start.37) | collective-permute-done | bytes 294944 | tf_op jit(solution)/shard_map/ppermute | solution.py:737
  (170 shorter events, 104.1 us)
Async XLA Ops:
  8.0 18.7 %collective-permute-start.3 = (bf16[136,768]{1,0:T(8,128)(2,1)S(1)}, bf16[136,768]{1,0:T(8,128)(2,1)S(1)}, u32[]{:S(2)}, u32[]{:S(2)}) collective-permute-start(bf16[136,768]{1,0:T(8,128)(2,1)S(1)} %pad_maximum_fusion.6), channel_id=1, source_target_pairs={{0,4},{1,12},{2,6},{3,14},{4,0},{5,8},{6,2},{7,10},{8,5},{9,13},{1... | collective-permute-start | bytes 626696 | tf_op jit(solution)/shard_map/ppermute | solution.py:532
  8.1 18.6 %collective-permute-start.2 = (bf16[136,768]{1,0:T(8,128)(2,1)S(1)}, bf16[136,768]{1,0:T(8,128)(2,1)S(1)}, u32[]{:S(2)}, u32[]{:S(2)}) collective-permute-start(bf16[136,768]{1,0:T(8,128)(2,1)S(1)} %pad_maximum_fusion.5), channel_id=1, source_target_pairs={{0,2},{1,10},{2,4},{3,12},{4,6},{5,14},{6,0},{7,8},{8,3},{9,11},{1... | collective-permute-start | bytes 626696 | tf_op jit(solution)/shard_map/ppermute | solution.py:532
  9.2 27.4 %collective-permute-start.1 = (bf16[136,768]{1,0:T(8,128)(2,1)S(1)}, bf16[136,768]{1,0:T(8,128)(2,1)S(1)}, u32[]{:S(2)}, u32[]{:S(2)}) collective-permute-start(bf16[136,768]{1,0:T(8,128)(2,1)S(1)} %pad_maximum_fusion.4), channel_id=1, source_target_pairs={{0,0},{1,8},{2,2},{3,10},{4,4},{5,12},{6,6},{7,14},{8,1},{9,9},{10... | collective-permute-start | bytes 626696 | tf_op jit(solution)/shard_map/ppermute | solution.py:532
  9.9 27.5 %collective-permute-start = (s32[4]{0:T(128)S(1)}, s32[4]{0:T(128)S(1)}, u32[]{:S(2)}, u32[]{:S(2)}) collective-permute-start(s32[4]{0:T(128)S(1)} %copy-done.18), channel_id=1, source_target_pairs={{0,8},{8,0},{16,24},{24,16},{1,9},{9,1},{17,25},{25,17},{2,10},{10... | collective-permute-start | bytes 56 | tf_op jit(solution)/shard_map/ppermute | solution.py:529
  14.8 26.9 %collective-permute-start.7 = (bf16[128,768]{1,0:T(8,128)(2,1)S(1)}, bf16[128,768]{1,0:T(8,128)(2,1)S(1)}, u32[]{:S(2)}, u32[]{:S(2)}) collective-permute-start(bf16[128,768]{1,0:T(8,128)(2,1)S(1)} %get-tuple-element.128), channel_id=1, source_target_pairs={{0,6},{1,14},{2,0},{3,8},{4,2},{5,10},{6,4},{7,12},{8,7},{9,15},{1... | collective-permute-start | bytes 589832 | tf_op jit(solution)/shard_map/ppermute | solution.py:532
  106.0 74.6 %collective-permute-start.33 = (bf16[2,3,8,96,512]{4,3,2,1,0:T(8,128)(2,1)}, bf16[2,3,8,96,512]{4,3,2,1,0:T(8,128)(2,1)}, u32[]{:S(2)}, u32[]{:S(2)}) collective-permute-start(bf16[2,3,8,96,512]{4,3,2,1,0:T(8,128)(2,1)} %get-tuple-element.104), channel_id=1, source_target_pairs={{0,8},{8,0},{16,24},{24,16},{1,9},{9,1},{17,25},{25,17},{2,10},{10... | collective-permute-start | bytes 14155784 | tf_op jit(solution)/shard_map/ppermute | solution.py:529
  125.6 48.9 %collective-permute-start.25 = (bf16[5,768,384]{2,1,0:T(8,128)(2,1)}, bf16[5,768,384]{2,1,0:T(8,128)(2,1)}, u32[]{:S(2)}, u32[]{:S(2)}) collective-permute-start(bf16[5,768,384]{2,1,0:T(8,128)(2,1)} %get-tuple-element.102), channel_id=1, source_target_pairs={{0,8},{8,0},{16,24},{24,16},{1,9},{9,1},{17,25},{25,17},{2,10},{10... | collective-permute-start | bytes 8847368 | tf_op jit(solution)/shard_map/ppermute | solution.py:529
  177.5 59.7 %collective-permute-start.26 = (bf16[5,2,2,96,384]{4,3,0,1,2:T(8,128)(2,1)}, bf16[5,2,2,96,384]{4,3,0,1,2:T(8,128)(2,1)}, u32[]{:S(2)}, u32[]{:S(2)}) collective-permute-start(bf16[5,2,2,96,384]{4,3,0,1,2:T(8,128)(2,1)} %fusion.1), channel_id=1, source_target_pairs={{0,1},{1,0},{2,3},{3,2},{4,5},{5,4},{6,7},{7,6},{8,9},{9,8},{10,11... | collective-permute-start | bytes 4423688 | tf_op jit(solution)/shard_map/ppermute | solution.py:737
  179.9 53.5 %collective-permute-start.22 = (bf16[2,2,96,1280]{3,2,1,0:T(8,128)(2,1)}, bf16[2,2,96,1280]{3,2,1,0:T(8,128)(2,1)S(1)}, u32[]{:S(2)}, u32[]{:S(2)}) collective-permute-start(bf16[2,2,96,1280]{3,2,1,0:T(8,128)(2,1)} %dynamic-slice_bitcast_fusion), channel_id=1, source_target_pairs={{0,1},{1,0},{2,3},{3,2},{4,5},{5,4},{6,7},{7,6},{8,9},{9,8},{10,11... | collective-permute-start | bytes 2949128 | tf_op jit(solution)/shard_map/ppermute | solution.py:737
  185.3 90.2 %collective-permute-start.34 = (bf16[3,8,96,512]{3,2,1,0:T(8,128)(2,1)}, bf16[3,8,96,512]{3,2,1,0:T(8,128)(2,1)}, u32[]{:S(2)}, u32[]{:S(2)}) collective-permute-start(bf16[3,8,96,512]{3,2,1,0:T(8,128)(2,1)} %fusion), channel_id=1, source_target_pairs={{0,16},{8,24},{16,0},{24,8},{1,17},{9,25},{17,1},{25,9},{2,18},{10... | collective-permute-start | bytes 7077896 | tf_op jit(solution)/shard_map/ppermute | solution.py:737
  186.9 50.3 %collective-permute-start.11 = (bf16[4,8,768]{2,1,0:T(8,128)(2,1)S(1)}, bf16[4,8,768]{2,1,0:T(8,128)(2,1)S(1)}, u32[]{:S(2)}, u32[]{:S(2)}) collective-permute-start(bf16[4,8,768]{2,1,0:T(8,128)(2,1)S(1)} %fusion.23), channel_id=1, source_target_pairs={{0,8},{8,0},{16,24},{24,16},{1,9},{9,1},{17,25},{25,17},{2,10},{10... | collective-permute-start | bytes 147464 | tf_op jit(solution)/shard_map/ppermute | solution.py:529
  186.9 57.5 %collective-permute-start.17 = (bf16[512,768]{1,0:T(8,128)(2,1)}, bf16[512,768]{1,0:T(8,128)(2,1)}, u32[]{:S(2)}, u32[]{:S(2)}) collective-permute-start(bf16[512,768]{1,0:T(8,128)(2,1)} %get-tuple-element.87), channel_id=1, source_target_pairs={{0,8},{8,0},{16,24},{24,16},{1,9},{9,1},{17,25},{25,17},{2,10},{10... | collective-permute-start | bytes 2359304 | tf_op jit(solution)/shard_map/ppermute | solution.py:529
  239.9 33.4 %collective-permute-start.27 = (bf16[5,2,96,384]{3,2,0,1:T(8,128)(2,1)}, bf16[5,2,96,384]{3,2,0,1:T(8,128)(2,1)}, u32[]{:S(2)}, u32[]{:S(2)}) collective-permute-start(bf16[5,2,96,384]{3,2,0,1:T(8,128)(2,1)} %fusion.2), channel_id=1, source_target_pairs={{0,2},{1,3},{2,0},{3,1},{4,6},{5,7},{6,4},{7,5},{8,10},{9,11},{10,... | collective-permute-start | bytes 2211848 | tf_op jit(solution)/shard_map/ppermute | solution.py:737
  241.0 69.5 %collective-permute-start.12 = (bf16[136,768]{1,0:T(8,128)(2,1)}, bf16[136,768]{1,0:T(8,128)(2,1)}, u32[]{:S(2)}, u32[]{:S(2)}) collective-permute-start(bf16[136,768]{1,0:T(8,128)(2,1)} %get-tuple-element.117), channel_id=1, source_target_pairs={{0,0},{1,8},{2,2},{3,10},{4,4},{5,12},{6,6},{7,14},{8,1},{9,9},{10... | collective-permute-start | bytes 626696 | tf_op jit(solution)/shard_map/ppermute | solution.py:532
  244.4 68.6 %collective-permute-start.13 = (bf16[136,768]{1,0:T(8,128)(2,1)}, bf16[136,768]{1,0:T(8,128)(2,1)}, u32[]{:S(2)}, u32[]{:S(2)}) collective-permute-start(bf16[136,768]{1,0:T(8,128)(2,1)} %get-tuple-element.118), channel_id=1, source_target_pairs={{0,2},{1,10},{2,4},{3,12},{4,6},{5,14},{6,0},{7,8},{8,3},{9,11},{1... | collective-permute-start | bytes 626696 | tf_op jit(solution)/shard_map/ppermute | solution.py:532
  252.3 63.1 %collective-permute-start.14 = (bf16[136,768]{1,0:T(8,128)(2,1)}, bf16[136,768]{1,0:T(8,128)(2,1)}, u32[]{:S(2)}, u32[]{:S(2)}) collective-permute-start(bf16[136,768]{1,0:T(8,128)(2,1)} %get-tuple-element.119), channel_id=1, source_target_pairs={{0,4},{1,12},{2,6},{3,14},{4,0},{5,8},{6,2},{7,10},{8,5},{9,13},{1... | collective-permute-start | bytes 626696 | tf_op jit(solution)/shard_map/ppermute | solution.py:532
  273.3 20.1 %collective-permute-start.24 = (bf16[96,1280]{1,0:T(8,128)(2,1)S(1)}, bf16[96,1280]{1,0:T(8,128)(2,1)S(1)}, u32[]{:S(2)}, u32[]{:S(2)}) collective-permute-start(bf16[96,1280]{1,0:T(8,128)(2,1)S(1)} %fusion.11), channel_id=1, source_target_pairs={{0,4},{1,5},{2,6},{3,7},{4,0},{5,1},{6,2},{7,3},{8,12},{9,13},{10,... | collective-permute-start | bytes 737288 | tf_op jit(solution)/shard_map/ppermute | solution.py:737
  275.5 25.8 %collective-permute-start.28 = (bf16[5,96,384]{2,1,0:T(8,128)(2,1)}, bf16[5,96,384]{2,1,0:T(8,128)(2,1)}, u32[]{:S(2)}, u32[]{:S(2)}) collective-permute-start(bf16[5,96,384]{2,1,0:T(8,128)(2,1)} %fusion.6), channel_id=1, source_target_pairs={{0,4},{1,5},{2,6},{3,7},{4,0},{5,1},{6,2},{7,3},{8,12},{9,13},{10,... | collective-permute-start | bytes 1105928 | tf_op jit(solution)/shard_map/ppermute | solution.py:737
  293.4 30.4 %collective-permute-start.35 = (bf16[3,2,2,96,512]{4,3,0,1,2:T(8,128)(2,1)}, bf16[3,2,2,96,512]{4,3,0,1,2:T(8,128)(2,1)}, u32[]{:S(2)}, u32[]{:S(2)}) collective-permute-start(bf16[3,2,2,96,512]{4,3,0,1,2:T(8,128)(2,1)} %fusion.3), channel_id=1, source_target_pairs={{0,1},{1,0},{2,3},{3,2},{4,5},{5,4},{6,7},{7,6},{8,9},{9,8},{10,11... | collective-permute-start | bytes 3538952 | tf_op jit(solution)/shard_map/ppermute | solution.py:737
  301.3 19.1 %collective-permute-start.15 = (bf16[136,768]{1,0:T(8,128)(2,1)S(1)}, bf16[136,768]{1,0:T(8,128)(2,1)}, u32[]{:S(2)}, u32[]{:S(2)}) collective-permute-start(bf16[136,768]{1,0:T(8,128)(2,1)S(1)} %get-tuple-element.116), channel_id=1, source_target_pairs={{0,6},{1,14},{2,0},{3,8},{4,2},{5,10},{6,4},{7,12},{8,7},{9,15},{1... | collective-permute-start | bytes 626696 | tf_op jit(solution)/shard_map/ppermute | solution.py:532
  313.0 33.1 %collective-permute-start.30 = (bf16[9,96,192]{2,1,0:T(8,128)(2,1)}, bf16[9,96,192]{2,1,0:T(8,128)(2,1)}, u32[]{:S(2)}, u32[]{:S(2)}) collective-permute-start(bf16[9,96,192]{2,1,0:T(8,128)(2,1)} %get-tuple-element.138), channel_id=1, source_target_pairs={{0,8},{8,24},{16,0},{24,16},{1,9},{9,25},{17,1},{25,17},{2,10},{10... | collective-permute-start | bytes 995336 | tf_op jit(solution)/shard_map/ppermute | solution.py:786
  315.4 30.7 %collective-permute-start.29 = (bf16[9,96,192]{2,1,0:T(8,128)(2,1)}, bf16[9,96,192]{2,1,0:T(8,128)(2,1)}, u32[]{:S(2)}, u32[]{:S(2)}) collective-permute-start(bf16[9,96,192]{2,1,0:T(8,128)(2,1)} %get-tuple-element.137), channel_id=1, source_target_pairs={{0,0},{8,16},{16,8},{24,24},{1,1},{9,17},{17,9},{25,25},{2,2},{10,... | collective-permute-start | bytes 995336 | tf_op jit(solution)/shard_map/ppermute | solution.py:786
  320.7 17.1 %collective-permute-start.20 = (bf16[128,768]{1,0:T(8,128)(2,1)}, bf16[128,768]{1,0:T(8,128)(2,1)}, u32[]{:S(2)}, u32[]{:S(2)}) collective-permute-start(bf16[128,768]{1,0:T(8,128)(2,1)} %get-tuple-element.123), channel_id=1, source_target_pairs={{0,4},{1,12},{2,6},{3,14},{4,0},{5,8},{6,2},{7,10},{8,5},{9,13},{1... | collective-permute-start | bytes 589832 | tf_op jit(solution)/shard_map/ppermute | solution.py:532
  330.1 19.5 %collective-permute-start.36 = (bf16[3,2,96,512]{3,2,0,1:T(8,128)(2,1)S(1)}, bf16[3,2,96,512]{3,2,0,1:T(8,128)(2,1)S(1)}, u32[]{:S(2)}, u32[]{:S(2)}) collective-permute-start(bf16[3,2,96,512]{3,2,0,1:T(8,128)(2,1)S(1)} %fusion.4), channel_id=1, source_target_pairs={{0,2},{1,3},{2,0},{3,1},{4,6},{5,7},{6,4},{7,5},{8,10},{9,11},{10,... | collective-permute-start | bytes 1769480 | tf_op jit(solution)/shard_map/ppermute | solution.py:737
  (36 other events, 288.3 us)
